TPU v7x, 512 devices: a whole 4x4x16 slice. The times are simulated.
512 devices in a mesh: row: 16 (over z), col: 32 (over y, x, core).
Axes of the slice: x: 4, y: 4, z: 16, core: 2. Of those that a mesh axis runs over, the one named last changes fastest.
Arguments:
- new_keys: bfloat16 [1024, 28672], P('col', 'row'), may hold values from -6 to 6
- precision: bfloat16 [28672, 28672], P('row', 'col'), may hold values from -0.03125 to 0.03125
- stored_keys: bfloat16 [32, 256, 28672], P('row', None, 'col'), may hold values from -0.03125 to 0.03125
- pair_batch: int32 [16, 24], replicated, may hold values from 0 to 31, as said below
- pair_count: int32 [16], replicated, may hold values from 8 to 24, as said below
- batch_length: int32 [32], replicated, may hold values from 64 to 256
- batch_slot: int32 [32], replicated, may hold values from 0 to 31, each once
Outputs:
- whitened: bfloat16 [1024, 28672], P('row', 'col')
- intersections: float32 [16, 24, 64, 256], P('row', None, 'col')
Inputs may be any that keep to these rules, and one draw needn't show every extreme that they name: `pair_batch`: the ids in one block's row are distinct; ids at places at or beyond the block's count are ignored. `pair_count`: some block lists exactly 24 batches. `batch_slot`: every store slot belongs to exactly one batch.
All inputs are finite; a program needn't handle non-finite values.
Results may differ from a plain program's by a relative error of at most 0.0029.
Values may be sent and summed in bfloat16 or wider, within the bound.
A program may use at most 64 MiB of HBM per device.

v0:
```python
import jax
import jax.numpy as jnp
from jax import lax
from jax.sharding import PartitionSpec as P


def against_store(rows, stored_keys):
    return jnp.einsum("kd,qjd->qkj", rows, stored_keys, preferred_element_type=jnp.float32)


def select_pairs(table, slots, lengths, count):
    picked = jnp.take(table, slots, axis=0)
    places = jnp.arange(slots.shape[0], dtype=jnp.int32)
    columns = jnp.arange(table.shape[-1], dtype=jnp.int32)
    keep = (places < count)[:, None, None] & (columns[None, None, :] < lengths[:, None, None])
    return jnp.where(keep, picked, jnp.zeros_like(picked))


def shards(new_keys, precision, stored_keys, pair_batch, pair_count, batch_length, batch_slot):
    row_count = lax.axis_size("row")
    col_count = lax.axis_size("col")
    row_index = lax.axis_index("row")
    total_keys = new_keys.shape[0] * col_count
    block_keys = total_keys // row_count
    partial_value = jnp.dot(
        lax.all_gather(new_keys, "col", axis=0, tiled=True),
        precision,
        preferred_element_type=jnp.float32,
    )
    every_row = lax.psum(partial_value, "row").astype(jnp.bfloat16)
    whitened = lax.dynamic_slice_in_dim(every_row, row_index * block_keys, block_keys, 0)
    terms = against_store(every_row, stored_keys)
    local_batches = terms.shape[0]
    batch_keys = terms.shape[2]
    blocks = terms.reshape(local_batches, row_count, block_keys, batch_keys)
    listed = pair_batch[row_index]
    slots = batch_slot[listed]
    lengths = batch_length[listed]
    count = pair_count[row_index]
    routed = lax.all_to_all(blocks, "row", split_axis=1, concat_axis=0, tiled=True)
    picked = select_pairs(routed[:, 0], slots, lengths, count)
    shares = lax.psum_scatter(picked, "col", scatter_dimension=1, tiled=True)
    return (whitened, shares[None])


def solution(mesh):
    placed = (P("col", "row"), P("row", "col"), P("row", None, "col"), P(), P(), P(), P())
    return jax.shard_map(
        shards,
        mesh=mesh,
        in_specs=placed,
        out_specs=(P("row", "col"), P("row", None, "col", None)),
        check_vma=False,
    )
```

profile of v0, /device:TPU:1, one launch (start us, length us, event | category | flops | bytes accessed | tf_op | source)
XLA Modules:
  0.0 392.9 jit_solution(3419381586753723229)
XLA Ops:
  7.2 0.0 copy-start
  7.2 0.0 all-gather.2.cloned.1.call-start
  7.2 0.7 all-gather.2.cloned.1.call-update
  7.9 69.9 %all-gather.2.cloned.1.call-done = bf16[1024,1792]{1,0:T(8,128)(2,1)} async-done(((bf16[32,1792]{1,0:T(8,128)(2,1)}), bf16[1024,1792]{1,0:T(8,128)(2,1)}) %all-gather.2.cloned.1.call-update) | async-done | bytes 3670032 | tf_op jit(solution)/shard_map/all_gather | solution.py:26
  77.8 0.0 copy-done
  77.8 7.8 %fusion.5 = f32[1024,896]{1,0:T(8,128)} fusion(bf16[1024,1792]{1,0:T(8,128)(2,1)} %all-gather.2.cloned.1.call-done, bf16[1792,896]{1,0:T(8,128)(2,1)S(1)} %copy-done), kind=kOutput, calls=%fused_computation.18 | convolution fusion | flops 3288334336 | bytes 10551296 | tf_op jit(solution)/shard_map/dot_general | solution.py:25
  85.6 87.3 %all-reduce.1 = bf16[1024,896]{1,0:T(8,128)(2,1)} all-reduce(f32[1024,896]{1,0:T(8,128)} %fusion.5), channel_id=1, replica_groups=mesh['row'=16,'col'=32] {'row'}, use_global_device_ids=true, to_apply=%region_0.0 | all-reduce | flops 917504 | bytes 5505024 | tf_op jit(solution)/shard_map/psum | solution.py:30
  172.9 3.0 fusion
  175.9 1.5 copy.10
  177.3 0.0 copy-start.1
  177.3 0.0 copy-start.2
  177.3 0.0 copy-start.3
  177.3 10.0 %all-to-all-start = ((f32[2,16,64,256]{3,2,0,1:T(8,128)}), f32[2,16,64,256]{3,2,0,1:T(8,128)}, u32[]{:S(2)}, u32[]{:S(2)}) async-start(f32[2,16,64,256]{3,2,0,1:T(8,128)} %copy.10), calls=%async_computation | async-start | bytes 4194304 | tf_op jit(solution)/shard_map/all_to_all | solution.py:40
  187.4 0.0 reduce-scatter.2.cloned.1.call-start
  187.4 0.7 fusion.3
  188.1 0.0 copy-done.1
  188.2 0.7 gather_fusion.1
  188.8 0.0 copy-done.2
  188.9 0.7 gather_fusion
  189.6 0.0 copy-done.3
  189.6 0.6 dynamic_slice.10
  190.2 0.6 iota_compare_fusion.1
  190.8 0.1 fusion.2
  190.9 88.4 %all-to-all-done = f32[2,16,64,256]{3,2,0,1:T(8,128)} async-done(((f32[2,16,64,256]{3,2,0,1:T(8,128)}), f32[2,16,64,256]{3,2,0,1:T(8,128)}, u32[]{:S(2)}, u32[]{:S(2)}) %all-to-all-start) | async-done | bytes 2097184 | tf_op jit(solution)/shard_map/all_to_all | solution.py:40
  279.3 3.4 gather_fusion.2
  282.7 1.6 select_select_fusion
  284.3 2.1 copy.11
  286.4 0.0 reduce-scatter.2.cloned.1.call-update
  286.4 1.6 constant_dynamic-slice_fusion
  287.9 96.7 %reduce-scatter.2.cloned.1.call-done = f32[24,2,256]{2,0,1:T(8,128)} async-done(((f32[24,64,256]{2,0,1:T(8,128)}), f32[24,2,256]{2,0,1:T(8,128)}) %reduce-scatter.2.cloned.1.call-update) | async-done | bytes 49168 | tf_op jit(solution)/shard_map/reduce_scatter | solution.py:42
  384.6 1.4 copy.12
  (4 shorter events, 0.0 us)
Async XLA Ops:
  7.2 70.6 %copy-start = (bf16[1792,896]{1,0:T(8,128)(2,1)S(1)}, bf16[1792,896]{1,0:T(8,128)(2,1)}, u32[]{:S(2)}) copy-start(bf16[1792,896]{1,0:T(8,128)(2,1)} %param.8) | copy-start | bytes 9633796
  7.2 70.6 %all-gather.2.cloned.1.call-start = ((), (), s32[]{:S(2)}) async-start(), calls=%async_computation.2 | async-start | bytes 3784704 | tf_op jit(solution)/shard_map/all_gather | solution.py:26
  177.3 10.8 %copy-start.1 = (s32[32]{0:T(128)S(1)}, s32[32]{0:T(128)}, u32[]{:S(2)}) copy-start(s32[32]{0:T(128)} %param.13) | copy-start | bytes 388
  177.3 11.5 %copy-start.2 = (s32[32]{0:T(128)S(1)}, s32[32]{0:T(128)}, u32[]{:S(2)}) copy-start(s32[32]{0:T(128)} %param.12) | copy-start | bytes 388
  177.3 12.2 %copy-start.3 = (s32[16]{0:T(128)S(1)}, s32[16]{0:T(128)}, u32[]{:S(2)}) copy-start(s32[16]{0:T(128)} %param.11) | copy-start | bytes 196
  177.3 101.9 %all-to-all-start = ((f32[2,16,64,256]{3,2,0,1:T(8,128)}), f32[2,16,64,256]{3,2,0,1:T(8,128)}, u32[]{:S(2)}, u32[]{:S(2)}) async-start(f32[2,16,64,256]{3,2,0,1:T(8,128)} %copy.10), calls=%async_computation | async-start | bytes 4194304 | tf_op jit(solution)/shard_map/all_to_all | solution.py:40
  187.4 197.3 %reduce-scatter.2.cloned.1.call-start = ((), (), s32[]{:S(2)}) async-start(), calls=%async_computation.3 | async-start | bytes 1622016 | tf_op jit(solution)/shard_map/reduce_scatter | solution.py:42
Sparse Core Ops, SparseCore 0:
  11.1 66.6 all-gather.1
  286.5 98.0 reduce-scatter.1
where the time goes:
time: 394 us; the launch traced here: 393 us
  waiting for transfers between devices  256 us (65%)
  blocking collectives  87.3 us (22%)
  between operations  14.1 us (4%)
  local copies, waits for them, and re-layouts  11.9 us (3%)
  matrix products  10.8 us (3%)
  starting transfers between devices  10.1 us (3%)
    reduce_scatter x1, waiting for transfers between devices, shards(): shares = lax.psum_scatter(picked, 'col', scatter_dimension=1, tiled=True)  96.7 us
    all_to_all x1, waiting for transfers between devices, shards(): lax.all_to_all(blocks, 'row', split_axis=1, concat_axis=0, tiled=True)  88.4 us
    psum x1, blocking collectives, shards(): every_row = lax.psum(partial_value, 'row').astype(jnp.bfloat16)  87.3 us
    all_gather x1, waiting for transfers between devices, shards(): lax.all_gather(new_keys, 'col', axis=0, tiled=True)  69.9 us
    all_to_all x1, starting transfers between devices, shards(): lax.all_to_all(blocks, 'row', split_axis=1, concat_axis=0, tiled=True)  10 us
  transfers between devices with their start and end apart: 3, of which 3 were waited for; matrix products, arithmetic and copies ran while one was open for 1% of the time, Pallas kernels for 0%

commit v1 on v0

v1 whole, which is shorter than its diff:
```python
import jax
import jax.numpy as jnp
from jax import lax
from jax.sharding import PartitionSpec as P


def shards(new_keys, precision, stored_keys, pair_batch, pair_count, batch_length, batch_slot):
    row_count = lax.axis_size("row")
    col_count = lax.axis_size("col")
    row_index = lax.axis_index("row")
    total_keys = new_keys.shape[0] * col_count
    block_keys = total_keys // row_count
    part_keys = block_keys // col_count
    local_batches, batch_keys, width = stored_keys.shape
    partial_value = jnp.dot(
        lax.all_gather(new_keys, "col", axis=0, tiled=True),
        precision,
        preferred_element_type=jnp.float32,
    )
    summed = lax.psum_scatter(partial_value, "row", scatter_dimension=0, tiled=True)
    whitened = summed.astype(jnp.bfloat16)
    every_row = lax.all_gather(whitened, "row", axis=0, tiled=True)
    rows = every_row.reshape(row_count, col_count, part_keys, width)
    terms = jnp.einsum("bcid,sjd->csbij", rows, stored_keys, preferred_element_type=jnp.float32)
    mine = lax.psum_scatter(terms, "col", scatter_dimension=0, tiled=True)[0]
    routed = lax.all_to_all(mine, "row", split_axis=1, concat_axis=0, tiled=True)
    table = routed[:, 0]
    listed = pair_batch[row_index]
    slots = batch_slot[listed]
    lengths = batch_length[listed]
    count = pair_count[row_index]
    picked = jnp.take(table, slots, axis=0)
    places = jnp.arange(slots.shape[0], dtype=jnp.int32)
    columns = jnp.arange(batch_keys, dtype=jnp.int32)
    keep = (places < count)[:, None, None] & (columns[None, None, :] < lengths[:, None, None])
    shares = jnp.where(keep, picked, jnp.zeros_like(picked))
    return (whitened, shares[None])


def solution(mesh):
    placed = (P("col", "row"), P("row", "col"), P("row", None, "col"), P(), P(), P(), P())
    return jax.shard_map(
        shards,
        mesh=mesh,
        in_specs=placed,
        out_specs=(P("row", "col"), P("row", None, "col", None)),
        check_vma=False,
    )
```

time: 394 us -> 380 us (0.964)
  blocking collectives: 87.3 us -> 0 us
  waiting for transfers between devices: 256 us -> 326 us
    psum x1 -> x0, blocking collectives: 87.3 us -> none  [shards(): every_row = lax.psum(partial_value, 'row').astype(jnp.bfloat16)]
    all_to_all x1, waiting for transfers between devices: 88.4 us -> 10.1 us  [shards(): lax.all_to_all(mine, 'row', split_axis=1, concat_axis=0, tiled=True)]
    reduce_scatter x1 -> x2, waiting for transfers between devices: 96.7 us -> 172 us  [the longest x1 104 us: shards(): mine = lax.psum_scatter(terms, 'col', scatter_dimension=0, tiled=True)[0]]
    all_gather x0 -> x1, waiting for transfers between devices: none -> 73 us  [shards(): every_row = lax.all_gather(whitened, 'row', axis=0, tiled=True)]
  transfers between devices with their start and end apart: 3 -> 5, of which waited for: 3 -> 5; matrix products, arithmetic and copies ran while one was open for 1% -> 1% of each run, Pallas kernels for 0% -> 0%
where the time goes in v1:
time: 380 us; the launch traced here: 378 us
  waiting for transfers between devices  326 us (86%)
  between operations  13.9 us (4%)
  starting transfers between devices  12.2 us (3%)
  local copies, waits for them, and re-layouts  11.5 us (3%)
  matrix products  10.8 us (3%)
    reduce_scatter x1, waiting for transfers between devices, shards(): mine = lax.psum_scatter(terms, 'col', scatter_dimension=0, tiled=True)[0]  104 us
    all_gather x1, waiting for transfers between devices, shards(): every_row = lax.all_gather(whitened, 'row', axis=0, tiled=True)  73 us
    all_gather x1, waiting for transfers between devices, shards(): lax.all_gather(new_keys, 'col', axis=0, tiled=True)  69.8 us
    reduce_scatter x1, waiting for transfers between devices, shards(): lax.psum_scatter(partial_value, 'row', scatter_dimension=0, tiled=True)  67.4 us
    all_to_all x1, starting transfers between devices, shards(): lax.all_to_all(mine, 'row', split_axis=1, concat_axis=0, tiled=True)  12 us
    all_to_all x1, waiting for transfers between devices, shards(): lax.all_to_all(mine, 'row', split_axis=1, concat_axis=0, tiled=True)  10.1 us
    dot_general x1, matrix products, shards(): jnp.dot(lax.all_gather(new_keys, 'col', axis=0, tiled=True), precision, p...  7.78 us
  transfers between devices with their start and end apart: 5, of which 5 were waited for; matrix products, arithmetic and copies ran while one was open for 1% of the time, Pallas kernels for 0%

profile of v1, /device:TPU:1, one launch (start us, length us, event | category | flops | bytes accessed | tf_op | source)
XLA Modules:
  0.0 377.6 jit_solution(4652722605744629083)
XLA Ops:
  7.2 0.0 copy-start
  7.2 0.0 all-gather.3.cloned.1.call-start
  7.2 0.7 all-gather.3.cloned.1.call-update
  7.9 0.0 reduce-scatter.3.cloned.1.call-start
  8.0 69.8 %all-gather.3.cloned.1.call-done = bf16[1024,1792]{1,0:T(8,128)(2,1)} async-done(((bf16[32,1792]{1,0:T(8,128)(2,1)}), bf16[1024,1792]{1,0:T(8,128)(2,1)}) %all-gather.3.cloned.1.call-update) | async-done | bytes 3670032 | tf_op jit(solution)/shard_map/all_gather | solution.py:16
  77.8 7.8 %fusion.10 = f32[1024,896]{1,0:T(8,128)} fusion(bf16[1024,1792]{1,0:T(8,128)(2,1)} %all-gather.3.cloned.1.call-done, bf16[1792,896]{1,0:T(8,128)(2,1)S(1)} %copy-done), kind=kOutput, calls=%fused_computation.20 | convolution fusion | flops 3288334336 | bytes 10551296 | tf_op jit(solution)/shard_map/dot_general | solution.py:15
  85.6 0.0 reduce-scatter.3.cloned.1.call-update
  85.6 0.0 all-gather.5.cloned.1.call-start
  85.7 67.4 %reduce-scatter.3.cloned.1.call-done = f32[64,896]{1,0:T(8,128)} async-done(((f32[1024,896]{1,0:T(8,128)}), f32[64,896]{1,0:T(8,128)}) %reduce-scatter.3.cloned.1.call-update) | async-done | bytes 229392 | tf_op jit(solution)/shard_map/reduce_scatter | solution.py:20
  153.1 1.6 convert_element_type.3
  154.7 0.0 all-gather.5.cloned.1.call-update
  154.7 0.0 reduce-scatter.5.cloned.1.call-start
  154.7 73.0 %all-gather.5.cloned.1.call-done = bf16[1024,896]{1,0:T(8,128)(2,1)} async-done(((bf16[64,896]{1,0:T(8,128)(2,1)}), bf16[1024,896]{1,0:T(8,128)(2,1)}) %all-gather.5.cloned.1.call-update) | async-done | bytes 1835024 | tf_op jit(solution)/shard_map/all_gather | solution.py:22
  227.7 4.8 %reshape.105 = bf16[16,32,2,896]{3,2,1,0:T(2,128)(2,1)} reshape(bf16[1024,896]{1,0:T(8,128)(2,1)} %all-gather.5.cloned.1.call-done) | data formatting | bytes 3670016 | tf_op jit(solution)/shard_map/reshape | solution.py:23
  232.5 3.0 fusion.2
  235.5 0.0 copy-start.3
  235.6 0.0 copy-start.1
  235.6 0.0 copy-start.2
  235.6 2.5 copy.16
  238.1 0.0 reduce-scatter.5.cloned.1.call-update
  238.2 0.6 dynamic_slice.6
  238.8 0.7 fusion.8
  239.5 0.7 gather_fusion.1
  240.2 104.4 %reduce-scatter.5.cloned.1.call-done = f32[1,2,16,2,256]{4,2,3,1,0:T(8,128)} async-done(((f32[32,2,16,2,256]{4,2,3,1,0:T(8,128)}), f32[1,2,16,2,256]{4,2,3,1,0:T(8,128)}) %reduce-scatter.5.cloned.1.call-update) | async-done | bytes 65552 | tf_op jit(solution)/shard_map/reduce_scatter | solution.py:25
  344.6 1.5 copy.17
  346.2 12.0 %all-to-all-start = ((f32[2,16,2,256]{3,2,0,1:T(2,128)}), f32[2,16,2,256]{3,2,0,1:T(2,128)S(1)}, u32[]{:S(2)}, u32[]{:S(2)}) async-start(f32[2,16,2,256]{3,2,0,1:T(2,128)} %copy.17), calls=%async_computation.2 | async-start | bytes 131072 | tf_op jit(solution)/shard_map/all_to_all | solution.py:26
  358.2 0.7 iota_compare_fusion.1
  358.9 0.7 gather_fusion
  359.6 0.1 fusion.7
  359.7 10.1 %all-to-all-done = f32[2,16,2,256]{3,2,0,1:T(2,128)S(1)} async-done(((f32[2,16,2,256]{3,2,0,1:T(2,128)}), f32[2,16,2,256]{3,2,0,1:T(2,128)S(1)}, u32[]{:S(2)}, u32[]{:S(2)}) %all-to-all-start) | async-done | bytes 65568 | tf_op jit(solution)/shard_map/all_to_all | solution.py:26
  369.8 0.6 gather_fusion.2
  370.4 0.7 fusion.6
  (8 shorter events, 0.0 us)
Async XLA Ops:
  7.2 70.6 %copy-start = (bf16[1792,896]{1,0:T(8,128)(2,1)S(1)}, bf16[1792,896]{1,0:T(8,128)(2,1)}, u32[]{:S(2)}) copy-start(bf16[1792,896]{1,0:T(8,128)(2,1)} %param.8) | copy-start | bytes 9633796
  7.2 70.6 %all-gather.3.cloned.1.call-start = ((), (), s32[]{:S(2)}) async-start(), calls=%async_computation.3 | async-start | bytes 3784704 | tf_op jit(solution)/shard_map/all_gather | solution.py:16
  7.9 145.1 %reduce-scatter.3.cloned.1.call-start = ((), (), s32[]{:S(2)}) async-start(), calls=%async_computation.4 | async-start | bytes 3899392 | tf_op jit(solution)/shard_map/reduce_scatter | solution.py:20
  85.6 142.1 %all-gather.5.cloned.1.call-start = ((), (), s32[]{:S(2)}) async-start(), calls=%async_computation.5 | async-start | bytes 1949696 | tf_op jit(solution)/shard_map/all_gather | solution.py:22
  154.7 190.0 %reduce-scatter.5.cloned.1.call-start = ((), (), s32[]{:S(2)}) async-start(), calls=%async_computation.6 | async-start | bytes 2162688 | tf_op jit(solution)/shard_map/reduce_scatter | solution.py:25
  235.5 2.6 copy-start.3
  235.6 3.9 %copy-start.1 = (s32[32]{0:T(128)S(1)}, s32[32]{0:T(128)}, u32[]{:S(2)}) copy-start(s32[32]{0:T(128)} %param.13) | copy-start | bytes 388
  235.6 123.3 %copy-start.2 = (s32[32]{0:T(128)S(1)}, s32[32]{0:T(128)}, u32[]{:S(2)}) copy-start(s32[32]{0:T(128)} %param.12) | copy-start | bytes 388
  346.2 23.6 %all-to-all-start = ((f32[2,16,2,256]{3,2,0,1:T(2,128)}), f32[2,16,2,256]{3,2,0,1:T(2,128)S(1)}, u32[]{:S(2)}, u32[]{:S(2)}) async-start(f32[2,16,2,256]{3,2,0,1:T(2,128)} %copy.17), calls=%async_computation.2 | async-start | bytes 131072 | tf_op jit(solution)/shard_map/all_to_all | solution.py:26
Sparse Core Ops, SparseCore 0:
  11.1 66.6 all-gather.2
  85.7 67.2 reduce-scatter.2
  155.7 71.9 all-gather.4
  238.3 106.3 reduce-scatter.4

commit v2 on v1

--- a/solution.py
+++ b/solution.py
@@ -1,7 +1,58 @@
+import functools
+
 import jax
 import jax.numpy as jnp
 from jax import lax
+from jax.experimental import pallas as pl
+from jax.experimental.pallas import tpu as pltpu
 from jax.sharding import PartitionSpec as P
+
+
+def _exchange_kernel(axis, other, n, gather, x_ref, out_ref, send_sems, recv_sems):
+    me = lax.axis_index(axis)
+    mine = lax.axis_index(other)
+
+    def at(peer):
+        return (peer, mine) if axis == "row" else (mine, peer)
+
+    barrier = pltpu.get_barrier_semaphore()
+    for d in range(1, n):
+        peer = lax.rem(me + d, n)
+        pl.semaphore_signal(barrier, inc=1, device_id=at(peer), device_id_type=pl.DeviceIdType.MESH)
+    pl.semaphore_wait(barrier, n - 1)
+    copies = []
+    for d in range(1, n):
+        peer = lax.rem(me + d, n)
+        src = x_ref if gather else x_ref.at[peer]
+        copy = pltpu.make_async_remote_copy(
+            src_ref=src, dst_ref=out_ref.at[me], send_sem=send_sems.at[d], recv_sem=recv_sems.at[d],
+            device_id=at(peer), device_id_type=pl.DeviceIdType.MESH)
+        copy.start()
+        copies.append(copy)
+    if gather:
+        out_ref[me] = x_ref[...]
+    else:
+        out_ref[me] = x_ref[me]
+    for d in range(1, n):
+        copies[d - 1].wait_send()
+        source = lax.rem(me + n - d, n)
+        src = x_ref if gather else x_ref.at[source]
+        incoming = pltpu.make_async_remote_copy(
+            src_ref=src, dst_ref=out_ref.at[source], send_sem=send_sems.at[d], recv_sem=recv_sems.at[d],
+            device_id=at(source), device_id_type=pl.DeviceIdType.MESH)
+        incoming.wait_recv()
+
+
+def exchange(x, axis, other, n, gather, collective_id):
+    block = x.shape if gather else x.shape[1:]
+    return pl.pallas_call(
+        functools.partial(_exchange_kernel, axis, other, n, gather),
+        out_shape=jax.ShapeDtypeStruct((n,) + tuple(block), x.dtype),
+        in_specs=[pl.BlockSpec(memory_space=pltpu.VMEM)],
+        out_specs=pl.BlockSpec(memory_space=pltpu.VMEM),
+        scratch_shapes=[pltpu.SemaphoreType.DMA((n,)), pltpu.SemaphoreType.DMA((n,))],
+        compiler_params=pltpu.CompilerParams(collective_id=collective_id, has_side_effects=True),
+    )(x)
 
 
 def shards(new_keys, precision, stored_keys, pair_batch, pair_count, batch_length, batch_slot):
@@ -12,8 +63,9 @@
     block_keys = total_keys // row_count
     part_keys = block_keys // col_count
     local_batches, batch_keys, width = stored_keys.shape
+    gathered = exchange(new_keys, "col", "row", col_count, True, 0)
     partial_value = jnp.dot(
-        lax.all_gather(new_keys, "col", axis=0, tiled=True),
+        gathered.reshape(total_keys, new_keys.shape[1]),
         precision,
         preferred_element_type=jnp.float32,
     )
@@ -22,9 +74,12 @@
     every_row = lax.all_gather(whitened, "row", axis=0, tiled=True)
     rows = every_row.reshape(row_count, col_count, part_keys, width)
     terms = jnp.einsum("bcid,sjd->csbij", rows, stored_keys, preferred_element_type=jnp.float32)
-    mine = lax.psum_scatter(terms, "col", scatter_dimension=0, tiled=True)[0]
-    routed = lax.all_to_all(mine, "row", split_axis=1, concat_axis=0, tiled=True)
-    table = routed[:, 0]
+    terms = terms.reshape(col_count, local_batches * row_count * part_keys, batch_keys)
+    mine = exchange(terms, "col", "row", col_count, False, 1).sum(0)
+    mine = mine.reshape(local_batches, row_count, part_keys, batch_keys).transpose(1, 0, 2, 3)
+    mine = mine.reshape(row_count, local_batches * part_keys, batch_keys)
+    routed = exchange(mine, "row", "col", row_count, False, 2)
+    table = routed.reshape(row_count * local_batches, part_keys, batch_keys)
     listed = pair_batch[row_index]
     slots = batch_slot[listed]
     lengths = batch_length[listed]

time: 380 us -> 321 us (0.84)
  waiting for transfers between devices: 326 us -> 136 us
  Pallas kernels: 0 us -> 138 us
  starting transfers between devices: 12.2 us -> 0.08 us
  local copies, waits for them, and re-layouts: 11.5 us -> 15.6 us
    pallas_call x0 -> x3, Pallas kernels: none -> 138 us  [exchange(): pl.pallas_call(functools.partial(_exchange_kernel, axis, other, n, gather...]
    reduce_scatter x1 -> x0, waiting for transfers between devices: 104 us -> none  [shards(): mine = lax.psum_scatter(terms, 'col', scatter_dimension=0, tiled=True)[0]]
    all_gather x1 -> x0, waiting for transfers between devices: 69.8 us -> none  [shards(): lax.all_gather(new_keys, 'col', axis=0, tiled=True)]
    all_to_all x1 -> x0, starting transfers between devices: 12 us -> none  [shards(): lax.all_to_all(mine, 'row', split_axis=1, concat_axis=0, tiled=True)]
    all_to_all x1 -> x0, waiting for transfers between devices: 10.1 us -> none  [shards(): lax.all_to_all(mine, 'row', split_axis=1, concat_axis=0, tiled=True)]
    reshape x0 -> x4, local copies, waits for them, and re-layouts: none -> 5.29 us  [the longest x1 3.69 us: shards(): terms.reshape(col_count, local_batches * row_count * part_keys, batch_keys)]
    all_gather x1, waiting for transfers between devices: 73 us -> 69 us  [shards(): every_row = lax.all_gather(whitened, 'row', axis=0, tiled=True)]
  transfers between devices with their start and end apart: 5 -> 2, of which waited for: 5 -> 2; matrix products, arithmetic and copies ran while one was open for 1% -> 1% of each run, Pallas kernels for 0% -> 0%
where the time goes in v2:
time: 321 us; the launch traced here: 320 us
  Pallas kernels  138 us (43%)
  waiting for transfers between devices  136 us (42%)
  local copies, waits for them, and re-layouts  15.6 us (5%)
  between operations  14.1 us (4%)
  matrix products  10.8 us (3%)
  other arithmetic  5.49 us (2%)
    pallas_call x3, Pallas kernels, exchange(): pl.pallas_call(functools.partial(_exchange_kernel, axis, other, n, gather...  138 us
    all_gather x1, waiting for transfers between devices, shards(): every_row = lax.all_gather(whitened, 'row', axis=0, tiled=True)  69 us
    reduce_scatter x1, waiting for transfers between devices, shards(): lax.psum_scatter(partial_value, 'row', scatter_dimension=0, tiled=True)  67.2 us
    dot_general x1, matrix products, shards(): jnp.dot(gathered.reshape(total_keys, new_keys.shape[1]), precision, prefe...  7.77 us
  transfers between devices with their start and end apart: 2, of which 2 were waited for; matrix products, arithmetic and copies ran while one was open for 1% of the time, Pallas kernels for 0%

profile of v2, /device:TPU:1, one launch (start us, length us, event | category | flops | bytes accessed | tf_op | source)
XLA Modules:
  0.0 320.2 jit_solution(3287460772547938865)
XLA Ops:
  7.2 0.0 copy-start
  7.2 0.0 reduce-scatter.2.cloned.1.call-start
  7.2 72.3 %shard_map.86 = bf16[32,32,1792]{2,1,0:T(8,128)(2,1)} custom-call(bf16[32,1792]{1,0:T(8,128)(2,1)} %x_ref.1), custom_call_target="tpu_custom_call" | custom-call | tf_op jit(solution)/shard_map/pallas_call | solution.py:48
  79.5 0.0 copy-done
  79.5 7.8 %fusion.10 = f32[1024,896]{1,0:T(8,128)} fusion(bf16[1024,1792]{1,0:T(8,128)(2,1)} %bitcast.25, bf16[1792,896]{1,0:T(8,128)(2,1)S(1)} %copy-done), kind=kOutput, calls=%fused_computation.20 | convolution fusion | flops 3288334336 | bytes 10551296 | tf_op jit(solution)/shard_map/dot_general | solution.py:67
  87.3 0.0 copy-start.1
  87.3 0.0 reduce-scatter.2.cloned.1.call-update
  87.3 0.0 all-gather.2.cloned.1.call-start
  87.4 67.2 %reduce-scatter.2.cloned.1.call-done = f32[64,896]{1,0:T(8,128)} async-done(((f32[1024,896]{1,0:T(8,128)}), f32[64,896]{1,0:T(8,128)}) %reduce-scatter.2.cloned.1.call-update) | async-done | bytes 229392 | tf_op jit(solution)/shard_map/reduce_scatter | solution.py:72
  154.6 1.6 convert_element_type.3
  156.2 0.0 all-gather.2.cloned.1.call-update
  156.2 0.7 fusion.8
  156.9 0.0 copy-done.1
  156.9 0.7 gather_fusion.1
  157.6 0.0 copy-done.2
  157.6 0.7 gather_fusion
  158.3 0.0 copy-done.3
  158.4 0.6 dynamic_slice.6
  158.9 0.6 iota_compare_fusion.1
  159.6 0.1 fusion.7
  159.7 69.0 %all-gather.2.cloned.1.call-done = bf16[1024,896]{1,0:T(8,128)(2,1)} async-done(((bf16[64,896]{1,0:T(8,128)(2,1)}), bf16[1024,896]{1,0:T(8,128)(2,1)}) %all-gather.2.cloned.1.call-update) | async-done | bytes 1835024 | tf_op jit(solution)/shard_map/all_gather | solution.py:74
  228.7 4.8 %reshape.120 = bf16[16,32,2,896]{3,2,1,0:T(2,128)(2,1)} reshape(bf16[1024,896]{1,0:T(8,128)(2,1)} %all-gather.2.cloned.1.call-done) | data formatting | bytes 3670016 | tf_op jit(solution)/shard_map/reshape | solution.py:75
  233.5 3.0 fusion.2
  236.5 2.9 copy.12
  239.4 3.7 %reshape.121.x_ref = f32[32,64,256]{2,1,0:T(8,128)} reshape(f32[32,2,16,2,256]{4,3,2,1,0:T(2,128)} %copy.12) | data formatting | bytes 4194304 | tf_op jit(solution)/shard_map/reshape | solution.py:77
  243.1 50.7 %shard_map.87 = f32[32,64,256]{2,1,0:T(8,128)} custom-call(f32[32,64,256]{2,1,0:T(8,128)} %reshape.121.x_ref), custom_call_target="tpu_custom_call" | custom-call | tf_op jit(solution)/shard_map/pallas_call | solution.py:48
  293.8 1.7 reduce_sum.9
  295.6 0.7 reshape.123.x_ref
  296.3 14.8 %shard_map.88 = f32[16,4,256]{2,1,0:T(4,128)} custom-call(f32[16,4,256]{2,1,0:T(4,128)} %reshape.123.x_ref), custom_call_target="tpu_custom_call" | custom-call | tf_op jit(solution)/shard_map/pallas_call | solution.py:48
  311.1 0.9 reshape.124
  312.0 0.6 gather_fusion.2
  312.6 0.7 fusion.6
  (8 shorter events, 0.1 us)
Async XLA Ops:
  7.2 72.3 %copy-start = (bf16[1792,896]{1,0:T(8,128)(2,1)S(1)}, bf16[1792,896]{1,0:T(8,128)(2,1)}, u32[]{:S(2)}) copy-start(bf16[1792,896]{1,0:T(8,128)(2,1)} %param.8) | copy-start | bytes 9633796
  7.2 147.4 %reduce-scatter.2.cloned.1.call-start = ((), (), s32[]{:S(2)}) async-start(), calls=%async_computation.1 | async-start | bytes 3899392 | tf_op jit(solution)/shard_map/reduce_scatter | solution.py:72
  87.3 69.6 %copy-start.1 = (s32[32]{0:T(128)S(1)}, s32[32]{0:T(128)}, u32[]{:S(2)}) copy-start(s32[32]{0:T(128)} %param.13) | copy-start | bytes 388
  87.3 70.4 %copy-start.2 = (s32[32]{0:T(128)S(1)}, s32[32]{0:T(128)}, u32[]{:S(2)}) copy-start(s32[32]{0:T(128)} %param.12) | copy-start | bytes 388
  87.3 71.1 %copy-start.3 = (s32[16]{0:T(128)S(1)}, s32[16]{0:T(128)}, u32[]{:S(2)}) copy-start(s32[16]{0:T(128)} %param.11) | copy-start | bytes 196
  87.3 141.4 %all-gather.2.cloned.1.call-start = ((), (), s32[]{:S(2)}) async-start(), calls=%async_computation.2 | async-start | bytes 1949696 | tf_op jit(solution)/shard_map/all_gather | solution.py:74
Sparse Core Ops, SparseCore 0:
  87.4 67.1 reduce-scatter.1
  157.3 71.3 all-gather.1

commit v3 on v2

--- a/solution.py
+++ b/solution.py
@@ -55,6 +55,96 @@
     )(x)
 
 
+def _ring_kernel(n, partial_ref, out_ref, recv_r, recv_l, acc_r, acc_l, rs_send, rs_recv, ag_send, ag_recv):
+    me = lax.axis_index("row")
+    mine = lax.axis_index("col")
+    right = lax.rem(me + 1, n)
+    left = lax.rem(me + n - 1, n)
+    steps_r = n // 2
+    steps_l = n - 1 - steps_r
+    barrier = pltpu.get_barrier_semaphore()
+    for peer in (left, right):
+        pl.semaphore_signal(barrier, inc=1, device_id=(peer, mine), device_id_type=pl.DeviceIdType.MESH)
+    pl.semaphore_wait(barrier, 2)
+
+    def send(src, dst, sems, k, peer):
+        copy = pltpu.make_async_remote_copy(
+            src_ref=src, dst_ref=dst, send_sem=sems.at[k], recv_sem=sems.at[k + n],
+            device_id=(peer, mine), device_id_type=pl.DeviceIdType.MESH)
+        copy.start()
+        return copy
+
+    sent = []
+    for s in range(steps_r):
+        d_r = lax.rem(me + steps_r - s, n)
+        if s == 0:
+            src = partial_ref.at[d_r]
+        else:
+            sent_r[s - 1].wait_recv()
+            acc_r[s - 1] = recv_r[s - 1] + partial_ref[d_r]
+            src = acc_r.at[s - 1]
+        c = send(src, recv_r.at[s], rs_send, s, right)
+        sent.append(c)
+        sent_r = sent_r + [c] if s else [c]
+        if s < steps_l:
+            d_l = lax.rem(me + n - steps_l + s, n)
+            if s == 0:
+                src = partial_ref.at[d_l]
+            else:
+                sent_l[s - 1].wait_recv()
+                acc_l[s - 1] = recv_l[s - 1] + partial_ref[d_l]
+                src = acc_l.at[s - 1]
+            c = send(src, recv_l.at[s], rs_send, n // 2 + s, left)
+            sent.append(c)
+            sent_l = sent_l + [c] if s else [c]
+    sent_r[-1].wait_recv()
+    sent_l[-1].wait_recv()
+    total = partial_ref[me] + recv_r[steps_r - 1] + recv_l[steps_l - 1]
+    out_ref[me] = total.astype(out_ref.dtype)
+
+    for t in range(steps_r):
+        b_r = lax.rem(me + n - t, n)
+        if t:
+            got_r[t - 1].wait_recv()
+        c = send(out_ref.at[b_r], out_ref.at[b_r], ag_send, t, right)
+        sent.append(c)
+        got_r = got_r + [c] if t else [c]
+        if t < steps_l:
+            b_l = lax.rem(me + t, n)
+            if t:
+                got_l[t - 1].wait_recv()
+            c = send(out_ref.at[b_l], out_ref.at[b_l], ag_send, n // 2 + t, left)
+            sent.append(c)
+            got_l = got_l + [c] if t else [c]
+    got_r[-1].wait_recv()
+    got_l[-1].wait_recv()
+    for c in sent:
+        c.wait_send()
+
+
+def row_ring(partial, n, collective_id):
+    blocks, rows, width = partial.shape
+    steps_r = n // 2
+    steps_l = n - 1 - steps_r
+    return pl.pallas_call(
+        functools.partial(_ring_kernel, n),
+        out_shape=jax.ShapeDtypeStruct((blocks, rows, width), jnp.bfloat16),
+        in_specs=[pl.BlockSpec(memory_space=pltpu.VMEM)],
+        out_specs=pl.BlockSpec(memory_space=pltpu.VMEM),
+        scratch_shapes=[
+            pltpu.VMEM((steps_r, rows, width), jnp.float32),
+            pltpu.VMEM((steps_l, rows, width), jnp.float32),
+            pltpu.VMEM((steps_r - 1, rows, width), jnp.float32),
+            pltpu.VMEM((steps_l - 1, rows, width), jnp.float32),
+            pltpu.SemaphoreType.DMA((2 * n,)),
+            pltpu.SemaphoreType.DMA((2 * n,)),
+            pltpu.SemaphoreType.DMA((2 * n,)),
+            pltpu.SemaphoreType.DMA((2 * n,)),
+        ],
+        compiler_params=pltpu.CompilerParams(collective_id=collective_id, has_side_effects=True),
+    )(partial)
+
+
 def shards(new_keys, precision, stored_keys, pair_batch, pair_count, batch_length, batch_slot):
     row_count = lax.axis_size("row")
     col_count = lax.axis_size("col")
@@ -69,9 +159,8 @@
         precision,
         preferred_element_type=jnp.float32,
     )
-    summed = lax.psum_scatter(partial_value, "row", scatter_dimension=0, tiled=True)
-    whitened = summed.astype(jnp.bfloat16)
-    every_row = lax.all_gather(whitened, "row", axis=0, tiled=True)
+    every_row = row_ring(partial_value.reshape(row_count, block_keys, -1), row_count, 3)
+    whitened = every_row[row_index]
     rows = every_row.reshape(row_count, col_count, part_keys, width)
     terms = jnp.einsum("bcid,sjd->csbij", rows, stored_keys, preferred_element_type=jnp.float32)
     terms = terms.reshape(col_count, local_batches * row_count * part_keys, batch_keys)

time: 321 us -> 259 us (0.81)
  waiting for transfers between devices: 136 us -> 0 us
  Pallas kernels: 138 us -> 226 us
  between operations: 14.1 us -> 0.77 us
    pallas_call x0 -> x1, Pallas kernels: none -> 86.2 us  [row_ring(): pl.pallas_call(functools.partial(_ring_kernel, n), out_shape=jax.ShapeDty...]
    all_gather x1 -> x0, waiting for transfers between devices: 69 us -> none  [shards(): every_row = lax.all_gather(whitened, 'row', axis=0, tiled=True)]
    reduce_scatter x1 -> x0, waiting for transfers between devices: 67.2 us -> none  [shards(): lax.psum_scatter(partial_value, 'row', scatter_dimension=0, tiled=True)]
  transfers between devices with their start and end apart: 2 -> 0, of which waited for: 2 -> 0; matrix products, arithmetic and copies ran while one was open for 1% -> 0% of each run, Pallas kernels for 0% -> 0%
where the time goes in v3:
time: 259 us; the launch traced here: 258 us
  Pallas kernels  226 us (87%)
  local copies, waits for them, and re-layouts  17.2 us (7%)
  matrix products  10.8 us (4%)
  other arithmetic  3.91 us (2%)
    pallas_call x3, Pallas kernels, exchange(): pl.pallas_call(functools.partial(_exchange_kernel, axis, other, n, gather...  140 us
    pallas_call x1, Pallas kernels, row_ring(): pl.pallas_call(functools.partial(_ring_kernel, n), out_shape=jax.ShapeDty...  86.2 us
    dot_general x1, matrix products, shards(): jnp.dot(gathered.reshape(total_keys, new_keys.shape[1]), precision, prefe...  7.77 us

profile of v3, /device:TPU:1, one launch (start us, length us, event | category | flops | bytes accessed | tf_op | source)
XLA Modules:
  0.0 258.5 jit_solution(7156643012829737665)
XLA Ops:
  0.6 0.0 copy-start
  0.6 72.3 %shard_map.86 = bf16[32,32,1792]{2,1,0:T(8,128)(2,1)} custom-call(bf16[32,1792]{1,0:T(8,128)(2,1)} %x_ref.1), custom_call_target="tpu_custom_call" | custom-call | tf_op jit(solution)/shard_map/pallas_call | solution.py:48
  73.0 0.0 copy-done
  73.0 7.8 %fusion.partial_ref = f32[16,64,896]{2,1,0:T(8,128)} fusion(bf16[16,64,1792]{2,1,0:T(8,128)(2,1)} %bitcast.29, bf16[1792,896]{1,0:T(8,128)(2,1)S(1)} %copy-done), kind=kOutput, calls=%fused_computation.3 | convolution fusion | flops 3288334336 | bytes 10551296 | tf_op jit(solution)/shard_map/dot_general | solution.py:157
  80.8 86.2 %shard_map.87 = bf16[16,64,896]{2,1,0:T(8,128)(2,1)} custom-call(f32[16,64,896]{2,1,0:T(8,128)} %fusion.partial_ref), custom_call_target="tpu_custom_call" | custom-call | tf_op jit(solution)/shard_map/pallas_call | solution.py:129
  167.0 1.6 dynamic-slice_bitcast_fusion
  168.5 4.8 %reshape.120 = bf16[16,32,2,896]{3,2,1,0:T(2,128)(2,1)} reshape(bf16[16,64,896]{2,1,0:T(8,128)(2,1)} %shard_map.87) | data formatting | bytes 3670016 | tf_op jit(solution)/shard_map/reshape | solution.py:164
  173.3 3.0 %fusion.4 = f32[32,2,16,2,256]{4,0,1,3,2:T(8,128)S(1)} fusion(bf16[16,32,2,896,1]{3,2,1,0,4:T(2,128)(2,1)} %bitcast.30, bf16[2,256,896]{2,1,0:T(8,128)(2,1)} %param.9), kind=kOutput, calls=%fused_computation.7 | convolution fusion | flops 939524096 | bytes 4849664 | tf_op jit(solution)/shard_map/bcid,sjd->csbij/dot_general | solution.py:165
  176.3 2.9 %copy.12 = f32[32,2,16,2,256]{4,3,2,1,0:T(2,128)} copy(f32[32,2,16,2,256]{4,0,1,3,2:T(8,128)S(1)} %fusion.4) | data formatting | bytes 4194304 | tf_op jit(solution)/shard_map/bcid,sjd->csbij/transpose | solution.py:165
  179.3 3.7 %reshape.121.x_ref = f32[32,64,256]{2,1,0:T(8,128)} reshape(f32[32,2,16,2,256]{4,3,2,1,0:T(2,128)} %copy.12) | data formatting | bytes 4194304 | tf_op jit(solution)/shard_map/reshape | solution.py:166
  183.0 53.2 %shard_map.88 = f32[32,64,256]{2,1,0:T(8,128)} custom-call(f32[32,64,256]{2,1,0:T(8,128)} %reshape.121.x_ref), custom_call_target="tpu_custom_call" | custom-call | tf_op jit(solution)/shard_map/pallas_call | solution.py:48
  236.2 0.0 copy-start.1
  236.2 0.0 copy-start.2
  236.2 0.0 copy-start.3
  236.2 1.7 reduce_sum.9
  238.0 0.7 reshape.123.x_ref
  238.7 14.1 %shard_map.89 = f32[16,4,256]{2,1,0:T(4,128)} custom-call(f32[16,4,256]{2,1,0:T(4,128)} %reshape.123.x_ref), custom_call_target="tpu_custom_call" | custom-call | tf_op jit(solution)/shard_map/pallas_call | solution.py:48
  252.7 0.9 reshape.124
  253.6 0.7 fusion.10
  254.3 0.0 copy-done.1
  254.3 0.7 gather_fusion.1
  255.1 0.6 gather_fusion.2
  255.7 0.0 copy-done.2
  255.7 0.7 gather_fusion
  256.4 0.0 copy-done.3
  256.4 0.6 dynamic_slice.10
  257.0 0.6 iota_compare_fusion.1
  257.7 0.1 fusion.9
  257.7 0.7 fusion.8
  (6 shorter events, 0.1 us)
Async XLA Ops:
  0.6 72.3 %copy-start = (bf16[1792,896]{1,0:T(8,128)(2,1)S(1)}, bf16[1792,896]{1,0:T(8,128)(2,1)}, u32[]{:S(2)}) copy-start(bf16[1792,896]{1,0:T(8,128)(2,1)} %param.8) | copy-start | bytes 9633796
  236.2 18.2 %copy-start.1 = (s32[32]{0:T(128)S(1)}, s32[32]{0:T(128)}, u32[]{:S(2)}) copy-start(s32[32]{0:T(128)} %param.13) | copy-start | bytes 388
  236.2 19.5 %copy-start.2 = (s32[32]{0:T(128)S(1)}, s32[32]{0:T(128)}, u32[]{:S(2)}) copy-start(s32[32]{0:T(128)} %param.12) | copy-start | bytes 388
  236.2 20.2 %copy-start.3 = (s32[16]{0:T(128)S(1)}, s32[16]{0:T(128)}, u32[]{:S(2)}) copy-start(s32[16]{0:T(128)} %param.11) | copy-start | bytes 196

commit v4 on v3

--- a/solution.py
+++ b/solution.py
@@ -55,6 +55,58 @@
     )(x)
 
 
+def _gather_kernel(n, x_ref, out_ref, send_sems, forward_sems, recv_sems):
+    me = lax.axis_index("col")
+    mine = lax.axis_index("row")
+    core = lax.rem(me, 2)
+    chip = me // 2
+    chips = n // 2
+    sibling = chip * 2 + 1 - core
+    peers = [lax.rem(chip + d, chips) * 2 + core for d in range(1, chips)]
+    barrier = pltpu.get_barrier_semaphore()
+    for peer in peers + [sibling]:
+        pl.semaphore_signal(barrier, inc=1, device_id=(mine, peer), device_id_type=pl.DeviceIdType.MESH)
+    pl.semaphore_wait(barrier, chips)
+
+    def copy(src, slot, sem, peer):
+        return pltpu.make_async_remote_copy(
+            src_ref=src, dst_ref=out_ref.at[slot], send_sem=sem, recv_sem=recv_sems.at[slot],
+            device_id=(mine, peer), device_id_type=pl.DeviceIdType.MESH)
+
+    sent = []
+    for d, peer in enumerate(peers + [sibling]):
+        c = copy(x_ref, me, send_sems.at[d], peer)
+        c.start()
+        sent.append(c)
+    out_ref[me] = x_ref[...]
+    for d, peer in enumerate(peers):
+        copy(x_ref, peer, send_sems.at[d], peer).wait_recv()
+        c = copy(out_ref.at[peer], peer, forward_sems.at[d], sibling)
+        c.start()
+        sent.append(c)
+    copy(x_ref, sibling, send_sems.at[0], sibling).wait_recv()
+    for d in range(1, chips):
+        far = lax.rem(chip + d, chips) * 2 + 1 - core
+        copy(x_ref, far, send_sems.at[0], sibling).wait_recv()
+    for c in sent:
+        c.wait_send()
+
+
+def col_gather(x, n, collective_id):
+    return pl.pallas_call(
+        functools.partial(_gather_kernel, n),
+        out_shape=jax.ShapeDtypeStruct((n,) + x.shape, x.dtype),
+        in_specs=[pl.BlockSpec(memory_space=pltpu.VMEM)],
+        out_specs=pl.BlockSpec(memory_space=pltpu.VMEM),
+        scratch_shapes=[
+            pltpu.SemaphoreType.DMA((n,)),
+            pltpu.SemaphoreType.DMA((n,)),
+            pltpu.SemaphoreType.DMA((n,)),
+        ],
+        compiler_params=pltpu.CompilerParams(collective_id=collective_id, has_side_effects=True),
+    )(x)
+
+
 def _ring_kernel(n, partial_ref, out_ref, recv_r, recv_l, acc_r, acc_l, rs_send, rs_recv, ag_send, ag_recv):
     me = lax.axis_index("row")
     mine = lax.axis_index("col")
@@ -153,7 +205,7 @@
     block_keys = total_keys // row_count
     part_keys = block_keys // col_count
     local_batches, batch_keys, width = stored_keys.shape
-    gathered = exchange(new_keys, "col", "row", col_count, True, 0)
+    gathered = col_gather(new_keys, col_count, 0)
     partial_value = jnp.dot(
         gathered.reshape(total_keys, new_keys.shape[1]),
         precision,

time: 259 us -> 229 us (0.88)
  Pallas kernels: 226 us -> 196 us
    pallas_call x3 -> x2, Pallas kernels: 140 us -> 67 us  [exchange(): pl.pallas_call(functools.partial(_exchange_kernel, axis, other, n, gather...]
    pallas_call x0 -> x1, Pallas kernels: none -> 39.1 us  [col_gather(): pl.pallas_call(functools.partial(_gather_kernel, n), out_shape=jax.ShapeD...]
    pallas_call x1, Pallas kernels: 86.2 us -> 89.5 us  [row_ring(): pl.pallas_call(functools.partial(_ring_kernel, n), out_shape=jax.ShapeDty...]
where the time goes in v4:
time: 229 us; the launch traced here: 228 us
  Pallas kernels  196 us (86%)
  local copies, waits for them, and re-layouts  17.2 us (8%)
  matrix products  10.8 us (5%)
  other arithmetic  3.91 us (2%)
    pallas_call x1, Pallas kernels, row_ring(): pl.pallas_call(functools.partial(_ring_kernel, n), out_shape=jax.ShapeDty...  89.5 us
    pallas_call x2, Pallas kernels, exchange(): pl.pallas_call(functools.partial(_exchange_kernel, axis, other, n, gather...  67 us
    pallas_call x1, Pallas kernels, col_gather(): pl.pallas_call(functools.partial(_gather_kernel, n), out_shape=jax.ShapeD...  39.1 us
    dot_general x1, matrix products, shards(): jnp.dot(gathered.reshape(total_keys, new_keys.shape[1]), precision, prefe...  7.77 us
    reshape x1, local copies, waits for them, and re-layouts, shards(): rows = every_row.reshape(row_count, col_count, part_keys, width)  4.8 us

profile of v4, /device:TPU:1, one launch (start us, length us, event | category | flops | bytes accessed | tf_op | source)
XLA Modules:
  0.0 228.3 jit_solution(9832153357141704008)
XLA Ops:
  0.6 0.0 copy-start
  0.6 39.1 %shard_map.86 = bf16[32,32,1792]{2,1,0:T(8,128)(2,1)} custom-call(bf16[32,1792]{1,0:T(8,128)(2,1)} %x_ref.1), custom_call_target="tpu_custom_call" | custom-call | tf_op jit(solution)/shard_map/pallas_call | solution.py:96
  39.7 0.0 copy-done
  39.8 7.8 %fusion.partial_ref = f32[16,64,896]{2,1,0:T(8,128)} fusion(bf16[16,64,1792]{2,1,0:T(8,128)(2,1)} %bitcast.29, bf16[1792,896]{1,0:T(8,128)(2,1)S(1)} %copy-done), kind=kOutput, calls=%fused_computation.3 | convolution fusion | flops 3288334336 | bytes 10551296 | tf_op jit(solution)/shard_map/dot_general | solution.py:209
  47.5 89.5 %shard_map.87 = bf16[16,64,896]{2,1,0:T(8,128)(2,1)} custom-call(f32[16,64,896]{2,1,0:T(8,128)} %fusion.partial_ref), custom_call_target="tpu_custom_call" | custom-call | tf_op jit(solution)/shard_map/pallas_call | solution.py:181
  137.1 1.6 dynamic-slice_bitcast_fusion
  138.6 4.8 %reshape.120 = bf16[16,32,2,896]{3,2,1,0:T(2,128)(2,1)} reshape(bf16[16,64,896]{2,1,0:T(8,128)(2,1)} %shard_map.87) | data formatting | bytes 3670016 | tf_op jit(solution)/shard_map/reshape | solution.py:216
  143.4 3.0 %fusion.4 = f32[32,2,16,2,256]{4,0,1,3,2:T(8,128)S(1)} fusion(bf16[16,32,2,896,1]{3,2,1,0,4:T(2,128)(2,1)} %bitcast.30, bf16[2,256,896]{2,1,0:T(8,128)(2,1)} %param.9), kind=kOutput, calls=%fused_computation.7 | convolution fusion | flops 939524096 | bytes 4849664 | tf_op jit(solution)/shard_map/bcid,sjd->csbij/dot_general | solution.py:217
  146.4 2.9 %copy.12 = f32[32,2,16,2,256]{4,3,2,1,0:T(2,128)} copy(f32[32,2,16,2,256]{4,0,1,3,2:T(8,128)S(1)} %fusion.4) | data formatting | bytes 4194304 | tf_op jit(solution)/shard_map/bcid,sjd->csbij/transpose | solution.py:217
  149.4 3.7 %reshape.121.x_ref = f32[32,64,256]{2,1,0:T(8,128)} reshape(f32[32,2,16,2,256]{4,3,2,1,0:T(2,128)} %copy.12) | data formatting | bytes 4194304 | tf_op jit(solution)/shard_map/reshape | solution.py:218
  153.1 51.6 %shard_map.88 = f32[32,64,256]{2,1,0:T(8,128)} custom-call(f32[32,64,256]{2,1,0:T(8,128)} %reshape.121.x_ref), custom_call_target="tpu_custom_call" | custom-call | tf_op jit(solution)/shard_map/pallas_call | solution.py:48
  204.6 0.0 copy-start.1
  204.6 0.0 copy-start.2
  204.7 0.0 copy-start.3
  204.7 1.7 reduce_sum.9
  206.5 0.7 reshape.123.x_ref
  207.1 15.4 %shard_map.89 = f32[16,4,256]{2,1,0:T(4,128)} custom-call(f32[16,4,256]{2,1,0:T(4,128)} %reshape.123.x_ref), custom_call_target="tpu_custom_call" | custom-call | tf_op jit(solution)/shard_map/pallas_call | solution.py:48
  222.6 0.9 reshape.124
  223.4 0.7 fusion.10
  224.2 0.0 copy-done.1
  224.2 0.7 gather_fusion.1
  224.9 0.6 gather_fusion.2
  225.5 0.0 copy-done.2
  225.5 0.7 gather_fusion
  226.2 0.0 copy-done.3
  226.2 0.6 dynamic_slice.10
  226.8 0.6 iota_compare_fusion.1
  227.5 0.1 fusion.9
  227.6 0.7 fusion.8
  (6 shorter events, 0.1 us)
Async XLA Ops:
  0.6 39.1 %copy-start = (bf16[1792,896]{1,0:T(8,128)(2,1)S(1)}, bf16[1792,896]{1,0:T(8,128)(2,1)}, u32[]{:S(2)}) copy-start(bf16[1792,896]{1,0:T(8,128)(2,1)} %param.8) | copy-start | bytes 9633796
  204.6 19.5 %copy-start.1 = (s32[32]{0:T(128)S(1)}, s32[32]{0:T(128)}, u32[]{:S(2)}) copy-start(s32[32]{0:T(128)} %param.13) | copy-start | bytes 388
  204.6 20.9 %copy-start.2 = (s32[32]{0:T(128)S(1)}, s32[32]{0:T(128)}, u32[]{:S(2)}) copy-start(s32[32]{0:T(128)} %param.12) | copy-start | bytes 388
  204.7 21.6 %copy-start.3 = (s32[16]{0:T(128)S(1)}, s32[16]{0:T(128)}, u32[]{:S(2)}) copy-start(s32[16]{0:T(128)} %param.11) | copy-start | bytes 196

commit v5 on v4

--- a/solution.py
+++ b/solution.py
@@ -107,6 +107,64 @@
     )(x)
 
 
+def _scatter_kernel(n, x_ref, out_ref, half, recv, acc, send_sems, recv_sems):
+    me = lax.axis_index("col")
+    mine = lax.axis_index("row")
+    core = lax.rem(me, 2)
+    chip = me // 2
+    chips = n // 2
+    sibling = chip * 2 + 1 - core
+    peers = [lax.rem(chip + d, chips) * 2 + core for d in range(1, chips)]
+    barrier = pltpu.get_barrier_semaphore()
+    for peer in peers + [sibling]:
+        pl.semaphore_signal(barrier, inc=1, device_id=(mine, peer), device_id_type=pl.DeviceIdType.MESH)
+    pl.semaphore_wait(barrier, chips)
+
+    swap = pltpu.make_async_remote_copy(
+        src_ref=x_ref.at[:, 1 - core], dst_ref=half, send_sem=send_sems.at[0], recv_sem=recv_sems.at[0],
+        device_id=(mine, sibling), device_id_type=pl.DeviceIdType.MESH)
+    swap.start()
+    swap.wait_recv()
+    acc[...] = x_ref[:, core] + half[...]
+    sent = [swap]
+    for d in range(1, chips):
+        target = lax.rem(chip + d, chips)
+        c = pltpu.make_async_remote_copy(
+            src_ref=acc.at[target], dst_ref=recv.at[chip], send_sem=send_sems.at[d], recv_sem=recv_sems.at[d],
+            device_id=(mine, target * 2 + core), device_id_type=pl.DeviceIdType.MESH)
+        c.start()
+        sent.append(c)
+    total = acc[chip]
+    for d in range(1, chips):
+        source = lax.rem(chip + chips - d, chips)
+        pltpu.make_async_remote_copy(
+            src_ref=acc.at[source], dst_ref=recv.at[source], send_sem=send_sems.at[d], recv_sem=recv_sems.at[d],
+            device_id=(mine, source * 2 + core), device_id_type=pl.DeviceIdType.MESH).wait_recv()
+        total = total + recv[source]
+    out_ref[...] = total
+    for c in sent:
+        c.wait_send()
+
+
+def col_scatter(x, n, collective_id):
+    chips = n // 2
+    block = x.shape[1:]
+    return pl.pallas_call(
+        functools.partial(_scatter_kernel, n),
+        out_shape=jax.ShapeDtypeStruct(block, x.dtype),
+        in_specs=[pl.BlockSpec(memory_space=pltpu.VMEM)],
+        out_specs=pl.BlockSpec(memory_space=pltpu.VMEM),
+        scratch_shapes=[
+            pltpu.VMEM((chips,) + block, x.dtype),
+            pltpu.VMEM((chips,) + block, x.dtype),
+            pltpu.VMEM((chips,) + block, x.dtype),
+            pltpu.SemaphoreType.DMA((chips,)),
+            pltpu.SemaphoreType.DMA((chips,)),
+        ],
+        compiler_params=pltpu.CompilerParams(collective_id=collective_id, has_side_effects=True),
+    )(x.reshape((chips, 2) + block))
+
+
 def _ring_kernel(n, partial_ref, out_ref, recv_r, recv_l, acc_r, acc_l, rs_send, rs_recv, ag_send, ag_recv):
     me = lax.axis_index("row")
     mine = lax.axis_index("col")
@@ -216,7 +274,7 @@
     rows = every_row.reshape(row_count, col_count, part_keys, width)
     terms = jnp.einsum("bcid,sjd->csbij", rows, stored_keys, preferred_element_type=jnp.float32)
     terms = terms.reshape(col_count, local_batches * row_count * part_keys, batch_keys)
-    mine = exchange(terms, "col", "row", col_count, False, 1).sum(0)
+    mine = col_scatter(terms, col_count, 1)
     mine = mine.reshape(local_batches, row_count, part_keys, batch_keys).transpose(1, 0, 2, 3)
     mine = mine.reshape(row_count, local_batches * part_keys, batch_keys)
     routed = exchange(mine, "row", "col", row_count, False, 2)

time: 229 us -> 210 us (0.917)
  Pallas kernels: 196 us -> 177 us
    pallas_call x2 -> x1, Pallas kernels: 67 us -> 15.5 us  [exchange(): pl.pallas_call(functools.partial(_exchange_kernel, axis, other, n, gather...]
    pallas_call x0 -> x1, Pallas kernels: none -> 33.5 us  [col_scatter(): pl.pallas_call(functools.partial(_scatter_kernel, n), out_shape=jax.Shape...]
    reshape x1 -> x0, local copies, waits for them, and re-layouts: 3.7 us -> none  [shards(): terms.reshape(col_count, local_batches * row_count * part_keys, batch_keys)]
    another operation x0 -> x1, local copies, waits for them, and re-layouts: none -> 3.69 us  [col_scatter(): x.reshape((chips, 2) + block)]
where the time goes in v5:
time: 210 us; the launch traced here: 209 us
  Pallas kernels  177 us (84%)
  local copies, waits for them, and re-layouts  18.1 us (9%)
  matrix products  10.8 us (5%)
  other arithmetic  2.18 us (1%)
    pallas_call x1, Pallas kernels, row_ring(): pl.pallas_call(functools.partial(_ring_kernel, n), out_shape=jax.ShapeDty...  89.2 us
    pallas_call x1, Pallas kernels, col_gather(): pl.pallas_call(functools.partial(_gather_kernel, n), out_shape=jax.ShapeD...  39.1 us
    pallas_call x1, Pallas kernels, col_scatter(): pl.pallas_call(functools.partial(_scatter_kernel, n), out_shape=jax.Shape...  33.5 us
    pallas_call x1, Pallas kernels, exchange(): pl.pallas_call(functools.partial(_exchange_kernel, axis, other, n, gather...  15.5 us
    dot_general x1, matrix products, shards(): jnp.dot(gathered.reshape(total_keys, new_keys.shape[1]), precision, prefe...  7.76 us
    reshape x1, local copies, waits for them, and re-layouts, shards(): rows = every_row.reshape(row_count, col_count, part_keys, width)  4.8 us

profile of v5, /device:TPU:1, one launch (start us, length us, event | category | flops | bytes accessed | tf_op | source)
XLA Modules:
  0.0 209.0 jit_solution(8036558603805970484)
XLA Ops:
  0.6 0.0 copy-start
  0.6 39.1 %shard_map.86 = bf16[32,32,1792]{2,1,0:T(8,128)(2,1)} custom-call(bf16[32,1792]{1,0:T(8,128)(2,1)} %x_ref.1), custom_call_target="tpu_custom_call" | custom-call | tf_op jit(solution)/shard_map/pallas_call | solution.py:96
  39.7 0.0 copy-done
  39.7 7.8 %fusion.partial_ref = f32[16,64,896]{2,1,0:T(8,128)} fusion(bf16[16,64,1792]{2,1,0:T(8,128)(2,1)} %bitcast.31, bf16[1792,896]{1,0:T(8,128)(2,1)S(1)} %copy-done), kind=kOutput, calls=%fused_computation.3 | convolution fusion | flops 3288334336 | bytes 10551296 | tf_op jit(solution)/shard_map/dot_general | solution.py:267
  47.5 89.2 %shard_map.87 = bf16[16,64,896]{2,1,0:T(8,128)(2,1)} custom-call(f32[16,64,896]{2,1,0:T(8,128)} %fusion.partial_ref), custom_call_target="tpu_custom_call" | custom-call | tf_op jit(solution)/shard_map/pallas_call | solution.py:239
  136.7 1.6 dynamic-slice_bitcast_fusion
  138.3 4.8 %reshape.117 = bf16[16,32,2,896]{3,2,1,0:T(2,128)(2,1)} reshape(bf16[16,64,896]{2,1,0:T(8,128)(2,1)} %shard_map.87) | data formatting | bytes 3670016 | tf_op jit(solution)/shard_map/reshape | solution.py:274
  143.1 3.0 %fusion.4 = f32[32,2,16,2,256]{4,0,1,3,2:T(8,128)S(1)} fusion(bf16[16,32,2,896,1]{3,2,1,0,4:T(2,128)(2,1)} %bitcast.32, bf16[2,256,896]{2,1,0:T(8,128)(2,1)} %param.9), kind=kOutput, calls=%fused_computation.7 | convolution fusion | flops 939524096 | bytes 4849664 | tf_op jit(solution)/shard_map/bcid,sjd->csbij/dot_general | solution.py:275
  146.1 2.9 %copy.13 = f32[32,2,16,2,256]{4,3,2,1,0:T(2,128)} copy(f32[32,2,16,2,256]{4,0,1,3,2:T(8,128)S(1)} %fusion.4) | data formatting | bytes 4194304 | tf_op jit(solution)/shard_map/bcid,sjd->csbij/transpose | solution.py:275
  149.0 3.7 %reshape_reshape.3.x_ref = f32[16,2,64,256]{3,2,1,0:T(8,128)} reshape(f32[32,2,16,2,256]{4,3,2,1,0:T(2,128)} %copy.13) | data formatting | bytes 4194304 | tf_op jit(solution)/shard_map/reshape;reshape | solution.py:165
  152.7 0.0 copy-start.1
  152.7 0.0 copy-start.2
  152.7 0.0 copy-start.3
  152.7 33.5 %shard_map.88 = f32[64,256]{1,0:T(8,128)} custom-call(f32[16,2,64,256]{3,2,1,0:T(8,128)} %reshape_reshape.3.x_ref), custom_call_target="tpu_custom_call" | custom-call | tf_op jit(solution)/shard_map/pallas_call | solution.py:152
  186.3 0.9 reshape.118
  187.2 0.7 reshape.119.x_ref
  187.8 15.5 %shard_map.89 = f32[16,4,256]{2,1,0:T(4,128)} custom-call(f32[16,4,256]{2,1,0:T(4,128)} %reshape.119.x_ref), custom_call_target="tpu_custom_call" | custom-call | tf_op jit(solution)/shard_map/pallas_call | solution.py:48
  203.3 0.9 reshape.120
  204.2 0.7 fusion.10
  204.9 0.0 copy-done.1
  204.9 0.7 gather_fusion.1
  205.6 0.6 gather_fusion.2
  206.3 0.0 copy-done.2
  206.3 0.7 gather_fusion
  207.0 0.0 copy-done.3
  207.0 0.6 dynamic_slice.10
  207.6 0.6 iota_compare_fusion.1
  208.2 0.1 fusion.9
  208.3 0.7 fusion.8
  (5 shorter events, 0.0 us)
Async XLA Ops:
  0.6 39.1 %copy-start = (bf16[1792,896]{1,0:T(8,128)(2,1)S(1)}, bf16[1792,896]{1,0:T(8,128)(2,1)}, u32[]{:S(2)}) copy-start(bf16[1792,896]{1,0:T(8,128)(2,1)} %param.8) | copy-start | bytes 9633796
  152.7 52.2 %copy-start.1 = (s32[32]{0:T(128)S(1)}, s32[32]{0:T(128)}, u32[]{:S(2)}) copy-start(s32[32]{0:T(128)} %param.13) | copy-start | bytes 388
  152.7 53.5 %copy-start.2 = (s32[32]{0:T(128)S(1)}, s32[32]{0:T(128)}, u32[]{:S(2)}) copy-start(s32[32]{0:T(128)} %param.12) | copy-start | bytes 388
  152.7 54.2 %copy-start.3 = (s32[16]{0:T(128)S(1)}, s32[16]{0:T(128)}, u32[]{:S(2)}) copy-start(s32[16]{0:T(128)} %param.11) | copy-start | bytes 196

commit v6 on v5

--- a/solution.py
+++ b/solution.py
@@ -165,13 +165,15 @@
     )(x.reshape((chips, 2) + block))
 
 
-def _ring_kernel(n, partial_ref, out_ref, recv_r, recv_l, acc_r, acc_l, rs_send, rs_recv, ag_send, ag_recv):
+def _ring_kernel(n, chunks, partial_ref, out_ref, recv_r, recv_l, acc_r, acc_l, rs_sems, ag_sems):
     me = lax.axis_index("row")
     mine = lax.axis_index("col")
     right = lax.rem(me + 1, n)
     left = lax.rem(me + n - 1, n)
     steps_r = n // 2
     steps_l = n - 1 - steps_r
+    size = partial_ref.shape[1] // chunks
+    half = n * chunks
     barrier = pltpu.get_barrier_semaphore()
     for peer in (left, right):
         pl.semaphore_signal(barrier, inc=1, device_id=(peer, mine), device_id_type=pl.DeviceIdType.MESH)
@@ -179,65 +181,72 @@
 
     def send(src, dst, sems, k, peer):
         copy = pltpu.make_async_remote_copy(
-            src_ref=src, dst_ref=dst, send_sem=sems.at[k], recv_sem=sems.at[k + n],
+            src_ref=src, dst_ref=dst, send_sem=sems.at[k], recv_sem=sems.at[k + 2 * half],
             device_id=(peer, mine), device_id_type=pl.DeviceIdType.MESH)
         copy.start()
         return copy
 
     sent = []
+    got_r = {}
+    got_l = {}
     for s in range(steps_r):
-        d_r = lax.rem(me + steps_r - s, n)
-        if s == 0:
-            src = partial_ref.at[d_r]
-        else:
-            sent_r[s - 1].wait_recv()
-            acc_r[s - 1] = recv_r[s - 1] + partial_ref[d_r]
-            src = acc_r.at[s - 1]
-        c = send(src, recv_r.at[s], rs_send, s, right)
-        sent.append(c)
-        sent_r = sent_r + [c] if s else [c]
-        if s < steps_l:
-            d_l = lax.rem(me + n - steps_l + s, n)
+        for h in range(chunks):
+            rows = pl.ds(h * size, size)
+            d_r = lax.rem(me + steps_r - s, n)
             if s == 0:
-                src = partial_ref.at[d_l]
+                src = partial_ref.at[d_r, rows]
             else:
-                sent_l[s - 1].wait_recv()
-                acc_l[s - 1] = recv_l[s - 1] + partial_ref[d_l]
-                src = acc_l.at[s - 1]
-            c = send(src, recv_l.at[s], rs_send, n // 2 + s, left)
-            sent.append(c)
-            sent_l = sent_l + [c] if s else [c]
-    sent_r[-1].wait_recv()
-    sent_l[-1].wait_recv()
-    total = partial_ref[me] + recv_r[steps_r - 1] + recv_l[steps_l - 1]
-    out_ref[me] = total.astype(out_ref.dtype)
-
+                got_r[s - 1, h].wait_recv()
+                acc_r[s - 1, rows] = recv_r[s - 1, rows] + partial_ref[d_r, rows]
+                src = acc_r.at[s - 1, rows]
+            got_r[s, h] = send(src, recv_r.at[s, rows], rs_sems, s * chunks + h, right)
+            sent.append(got_r[s, h])
+            if s < steps_l:
+                d_l = lax.rem(me + n - steps_l + s, n)
+                if s == 0:
+                    src = partial_ref.at[d_l, rows]
+                else:
+                    got_l[s - 1, h].wait_recv()
+                    acc_l[s - 1, rows] = recv_l[s - 1, rows] + partial_ref[d_l, rows]
+                    src = acc_l.at[s - 1, rows]
+                got_l[s, h] = send(src, recv_l.at[s, rows], rs_sems, half + s * chunks + h, left)
+                sent.append(got_l[s, h])
+    for h in range(chunks):
+        rows = pl.ds(h * size, size)
+        got_r[steps_r - 1, h].wait_recv()
+        got_l[steps_l - 1, h].wait_recv()
+        total = partial_ref[me, rows] + recv_r[steps_r - 1, rows] + recv_l[steps_l - 1, rows]
+        out_ref[me, rows] = total.astype(out_ref.dtype)
+
+    ag_r = {}
+    ag_l = {}
     for t in range(steps_r):
-        b_r = lax.rem(me + n - t, n)
-        if t:
-            got_r[t - 1].wait_recv()
-        c = send(out_ref.at[b_r], out_ref.at[b_r], ag_send, t, right)
-        sent.append(c)
-        got_r = got_r + [c] if t else [c]
-        if t < steps_l:
-            b_l = lax.rem(me + t, n)
+        for h in range(chunks):
+            rows = pl.ds(h * size, size)
+            b_r = lax.rem(me + n - t, n)
             if t:
-                got_l[t - 1].wait_recv()
-            c = send(out_ref.at[b_l], out_ref.at[b_l], ag_send, n // 2 + t, left)
-            sent.append(c)
-            got_l = got_l + [c] if t else [c]
-    got_r[-1].wait_recv()
-    got_l[-1].wait_recv()
+                ag_r[t - 1, h].wait_recv()
+            ag_r[t, h] = send(out_ref.at[b_r, rows], out_ref.at[b_r, rows], ag_sems, t * chunks + h, right)
+            sent.append(ag_r[t, h])
+            if t < steps_l:
+                b_l = lax.rem(me + t, n)
+                if t:
+                    ag_l[t - 1, h].wait_recv()
+                ag_l[t, h] = send(out_ref.at[b_l, rows], out_ref.at[b_l, rows], ag_sems, half + t * chunks + h, left)
+                sent.append(ag_l[t, h])
+    for h in range(chunks):
+        ag_r[steps_r - 1, h].wait_recv()
+        ag_l[steps_l - 1, h].wait_recv()
     for c in sent:
         c.wait_send()
 
 
-def row_ring(partial, n, collective_id):
+def row_ring(partial, n, collective_id, chunks=2):
     blocks, rows, width = partial.shape
     steps_r = n // 2
     steps_l = n - 1 - steps_r
     return pl.pallas_call(
-        functools.partial(_ring_kernel, n),
+        functools.partial(_ring_kernel, n, chunks),
         out_shape=jax.ShapeDtypeStruct((blocks, rows, width), jnp.bfloat16),
         in_specs=[pl.BlockSpec(memory_space=pltpu.VMEM)],
         out_specs=pl.BlockSpec(memory_space=pltpu.VMEM),
@@ -246,10 +255,8 @@
             pltpu.VMEM((steps_l, rows, width), jnp.float32),
             pltpu.VMEM((steps_r - 1, rows, width), jnp.float32),
             pltpu.VMEM((steps_l - 1, rows, width), jnp.float32),
-            pltpu.SemaphoreType.DMA((2 * n,)),
-            pltpu.SemaphoreType.DMA((2 * n,)),
-            pltpu.SemaphoreType.DMA((2 * n,)),
-            pltpu.SemaphoreType.DMA((2 * n,)),
+            pltpu.SemaphoreType.DMA((4 * n * chunks,)),
+            pltpu.SemaphoreType.DMA((4 * n * chunks,)),
         ],
         compiler_params=pltpu.CompilerParams(collective_id=collective_id, has_side_effects=True),
     )(partial)

time: 210 us -> 196 us (0.933)
  Pallas kernels: 177 us -> 164 us
    pallas_call x1, Pallas kernels: 89.2 us -> 80.5 us  [row_ring(): pl.pallas_call(functools.partial(_ring_kernel, n, chunks), out_shape=jax....]
    pallas_call x1, Pallas kernels: 33.5 us -> 30.2 us  [col_scatter(): pl.pallas_call(functools.partial(_scatter_kernel, n), out_shape=jax.Shape...]
where the time goes in v6:
time: 196 us
  Pallas kernels  164 us (84%)
  local copies, waits for them, and re-layouts  18.1 us (9%)
  matrix products  10.8 us (6%)
  other arithmetic  2.18 us (1%)
    pallas_call x1, Pallas kernels, row_ring(): pl.pallas_call(functools.partial(_ring_kernel, n, chunks), out_shape=jax....  80.5 us
    pallas_call x1, Pallas kernels, col_gather(): pl.pallas_call(functools.partial(_gather_kernel, n), out_shape=jax.ShapeD...  39.1 us
    pallas_call x1, Pallas kernels, col_scatter(): pl.pallas_call(functools.partial(_scatter_kernel, n), out_shape=jax.Shape...  30.2 us
    pallas_call x1, Pallas kernels, exchange(): pl.pallas_call(functools.partial(_exchange_kernel, axis, other, n, gather...  14.2 us
    dot_general x1, matrix products, shards(): jnp.dot(gathered.reshape(total_keys, new_keys.shape[1]), precision, prefe...  7.76 us
    reshape x1, local copies, waits for them, and re-layouts, shards(): rows = every_row.reshape(row_count, col_count, part_keys, width)  4.8 us

profile of v6, /device:TPU:1, one launch (start us, length us, event | category | flops | bytes accessed | tf_op | source)
XLA Modules:
  0.0 195.8 jit_solution(17229728131877691538)
XLA Ops:
  0.6 0.0 copy-start
  0.6 39.1 %shard_map.86 = bf16[32,32,1792]{2,1,0:T(8,128)(2,1)} custom-call(bf16[32,1792]{1,0:T(8,128)(2,1)} %x_ref.1), custom_call_target="tpu_custom_call" | custom-call | tf_op jit(solution)/shard_map/pallas_call | solution.py:96
  39.7 0.0 copy-done
  39.7 7.8 %fusion.partial_ref = f32[16,64,896]{2,1,0:T(8,128)} fusion(bf16[16,64,1792]{2,1,0:T(8,128)(2,1)} %bitcast.31, bf16[1792,896]{1,0:T(8,128)(2,1)S(1)} %copy-done), kind=kOutput, calls=%fused_computation.3 | convolution fusion | flops 3288334336 | bytes 10551296 | tf_op jit(solution)/shard_map/dot_general | solution.py:274
  47.5 80.5 %shard_map.87 = bf16[16,64,896]{2,1,0:T(8,128)(2,1)} custom-call(f32[16,64,896]{2,1,0:T(8,128)} %fusion.partial_ref), custom_call_target="tpu_custom_call" | custom-call | tf_op jit(solution)/shard_map/pallas_call | solution.py:248
  128.0 1.6 dynamic-slice_bitcast_fusion
  129.6 4.8 %reshape.117 = bf16[16,32,2,896]{3,2,1,0:T(2,128)(2,1)} reshape(bf16[16,64,896]{2,1,0:T(8,128)(2,1)} %shard_map.87) | data formatting | bytes 3670016 | tf_op jit(solution)/shard_map/reshape | solution.py:281
  134.4 3.0 %fusion.4 = f32[32,2,16,2,256]{4,0,1,3,2:T(8,128)S(1)} fusion(bf16[16,32,2,896,1]{3,2,1,0,4:T(2,128)(2,1)} %bitcast.32, bf16[2,256,896]{2,1,0:T(8,128)(2,1)} %param.9), kind=kOutput, calls=%fused_computation.7 | convolution fusion | flops 939524096 | bytes 4849664 | tf_op jit(solution)/shard_map/bcid,sjd->csbij/dot_general | solution.py:282
  137.4 2.9 %copy.13 = f32[32,2,16,2,256]{4,3,2,1,0:T(2,128)} copy(f32[32,2,16,2,256]{4,0,1,3,2:T(8,128)S(1)} %fusion.4) | data formatting | bytes 4194304 | tf_op jit(solution)/shard_map/bcid,sjd->csbij/transpose | solution.py:282
  140.3 3.7 %reshape_reshape.3.x_ref = f32[16,2,64,256]{3,2,1,0:T(8,128)} reshape(f32[32,2,16,2,256]{4,3,2,1,0:T(2,128)} %copy.13) | data formatting | bytes 4194304 | tf_op jit(solution)/shard_map/reshape;reshape | solution.py:165
  144.0 0.0 copy-start.1
  144.0 0.0 copy-start.2
  144.0 0.0 copy-start.3
  144.0 30.2 %shard_map.88 = f32[64,256]{1,0:T(8,128)} custom-call(f32[16,2,64,256]{3,2,1,0:T(8,128)} %reshape_reshape.3.x_ref), custom_call_target="tpu_custom_call" | custom-call | tf_op jit(solution)/shard_map/pallas_call | solution.py:152
  174.3 0.9 reshape.118
  175.2 0.7 reshape.119.x_ref
  175.8 14.2 %shard_map.89 = f32[16,4,256]{2,1,0:T(4,128)} custom-call(f32[16,4,256]{2,1,0:T(4,128)} %reshape.119.x_ref), custom_call_target="tpu_custom_call" | custom-call | tf_op jit(solution)/shard_map/pallas_call | solution.py:48
  190.0 0.9 reshape.120
  190.9 0.7 fusion.10
  191.6 0.0 copy-done.1
  191.7 0.7 gather_fusion.1
  192.4 0.6 gather_fusion.2
  193.0 0.0 copy-done.2
  193.0 0.7 gather_fusion
  193.7 0.0 copy-done.3
  193.7 0.6 dynamic_slice.10
  194.3 0.6 iota_compare_fusion.1
  195.0 0.1 fusion.9
  195.0 0.7 fusion.8
  (5 shorter events, 0.0 us)
Async XLA Ops:
  0.6 39.1 %copy-start = (bf16[1792,896]{1,0:T(8,128)(2,1)S(1)}, bf16[1792,896]{1,0:T(8,128)(2,1)}, u32[]{:S(2)}) copy-start(bf16[1792,896]{1,0:T(8,128)(2,1)} %param.8) | copy-start | bytes 9633796
  144.0 47.6 %copy-start.1 = (s32[32]{0:T(128)S(1)}, s32[32]{0:T(128)}, u32[]{:S(2)}) copy-start(s32[32]{0:T(128)} %param.13) | copy-start | bytes 388
  144.0 49.0 %copy-start.2 = (s32[32]{0:T(128)S(1)}, s32[32]{0:T(128)}, u32[]{:S(2)}) copy-start(s32[32]{0:T(128)} %param.12) | copy-start | bytes 388
  144.0 49.7 %copy-start.3 = (s32[16]{0:T(128)S(1)}, s32[16]{0:T(128)}, u32[]{:S(2)}) copy-start(s32[16]{0:T(128)} %param.11) | copy-start | bytes 196

commit v7 on v6

--- a/solution.py
+++ b/solution.py
@@ -241,7 +241,7 @@
         c.wait_send()
 
 
-def row_ring(partial, n, collective_id, chunks=2):
+def row_ring(partial, n, collective_id, chunks=4):
     blocks, rows, width = partial.shape
     steps_r = n // 2
     steps_l = n - 1 - steps_r

time: 196 us -> 196 us (level)
  no operation moved by 1% of the time
where the time goes in v7:
time: 196 us; the launch traced here: 195 us
  Pallas kernels  164 us (84%)
  local copies, waits for them, and re-layouts  18.1 us (9%)
  matrix products  10.8 us (6%)
  other arithmetic  2.18 us (1%)
    pallas_call x1, Pallas kernels, row_ring(): pl.pallas_call(functools.partial(_ring_kernel, n, chunks), out_shape=jax....  81.9 us
    pallas_call x1, Pallas kernels, col_gather(): pl.pallas_call(functools.partial(_gather_kernel, n), out_shape=jax.ShapeD...  39.1 us
    pallas_call x1, Pallas kernels, col_scatter(): pl.pallas_call(functools.partial(_scatter_kernel, n), out_shape=jax.Shape...  28.5 us
    pallas_call x1, Pallas kernels, exchange(): pl.pallas_call(functools.partial(_exchange_kernel, axis, other, n, gather...  14 us
    dot_general x1, matrix products, shards(): jnp.dot(gathered.reshape(total_keys, new_keys.shape[1]), precision, prefe...  7.76 us
    reshape x1, local copies, waits for them, and re-layouts, shards(): rows = every_row.reshape(row_count, col_count, part_keys, width)  4.8 us

profile of v7, /device:TPU:1, one launch (start us, length us, event | category | flops | bytes accessed | tf_op | source)
XLA Modules:
  0.0 195.3 jit_solution(12187239015524884976)
XLA Ops:
  0.6 0.0 copy-start
  0.6 39.1 %shard_map.86 = bf16[32,32,1792]{2,1,0:T(8,128)(2,1)} custom-call(bf16[32,1792]{1,0:T(8,128)(2,1)} %x_ref.1), custom_call_target="tpu_custom_call" | custom-call | tf_op jit(solution)/shard_map/pallas_call | solution.py:96
  39.7 0.0 copy-done
  39.7 7.8 %fusion.partial_ref = f32[16,64,896]{2,1,0:T(8,128)} fusion(bf16[16,64,1792]{2,1,0:T(8,128)(2,1)} %bitcast.31, bf16[1792,896]{1,0:T(8,128)(2,1)S(1)} %copy-done), kind=kOutput, calls=%fused_computation.3 | convolution fusion | flops 3288334336 | bytes 10551296 | tf_op jit(solution)/shard_map/dot_general | solution.py:274
  47.5 81.9 %shard_map.87 = bf16[16,64,896]{2,1,0:T(8,128)(2,1)} custom-call(f32[16,64,896]{2,1,0:T(8,128)} %fusion.partial_ref), custom_call_target="tpu_custom_call" | custom-call | tf_op jit(solution)/shard_map/pallas_call | solution.py:248
  129.4 1.6 dynamic-slice_bitcast_fusion
  131.0 4.8 %reshape.117 = bf16[16,32,2,896]{3,2,1,0:T(2,128)(2,1)} reshape(bf16[16,64,896]{2,1,0:T(8,128)(2,1)} %shard_map.87) | data formatting | bytes 3670016 | tf_op jit(solution)/shard_map/reshape | solution.py:281
  135.8 3.0 %fusion.4 = f32[32,2,16,2,256]{4,0,1,3,2:T(8,128)S(1)} fusion(bf16[16,32,2,896,1]{3,2,1,0,4:T(2,128)(2,1)} %bitcast.32, bf16[2,256,896]{2,1,0:T(8,128)(2,1)} %param.9), kind=kOutput, calls=%fused_computation.7 | convolution fusion | flops 939524096 | bytes 4849664 | tf_op jit(solution)/shard_map/bcid,sjd->csbij/dot_general | solution.py:282
  138.8 2.9 %copy.13 = f32[32,2,16,2,256]{4,3,2,1,0:T(2,128)} copy(f32[32,2,16,2,256]{4,0,1,3,2:T(8,128)S(1)} %fusion.4) | data formatting | bytes 4194304 | tf_op jit(solution)/shard_map/bcid,sjd->csbij/transpose | solution.py:282
  141.7 3.7 %reshape_reshape.3.x_ref = f32[16,2,64,256]{3,2,1,0:T(8,128)} reshape(f32[32,2,16,2,256]{4,3,2,1,0:T(2,128)} %copy.13) | data formatting | bytes 4194304 | tf_op jit(solution)/shard_map/reshape;reshape | solution.py:165
  145.4 0.0 copy-start.1
  145.4 0.0 copy-start.2
  145.4 0.0 copy-start.3
  145.4 28.5 %shard_map.88 = f32[64,256]{1,0:T(8,128)} custom-call(f32[16,2,64,256]{3,2,1,0:T(8,128)} %reshape_reshape.3.x_ref), custom_call_target="tpu_custom_call" | custom-call | tf_op jit(solution)/shard_map/pallas_call | solution.py:152
  174.0 0.9 reshape.118
  174.9 0.7 reshape.119.x_ref
  175.6 14.0 %shard_map.89 = f32[16,4,256]{2,1,0:T(4,128)} custom-call(f32[16,4,256]{2,1,0:T(4,128)} %reshape.119.x_ref), custom_call_target="tpu_custom_call" | custom-call | tf_op jit(solution)/shard_map/pallas_call | solution.py:48
  189.6 0.9 reshape.120
  190.5 0.7 fusion.10
  191.2 0.0 copy-done.1
  191.2 0.7 gather_fusion.1
  191.9 0.6 gather_fusion.2
  192.6 0.0 copy-done.2
  192.6 0.7 gather_fusion
  193.3 0.0 copy-done.3
  193.3 0.6 dynamic_slice.10
  193.9 0.6 iota_compare_fusion.1
  194.5 0.1 fusion.9
  194.6 0.7 fusion.8
  (5 shorter events, 0.0 us)
Async XLA Ops:
  0.6 39.1 %copy-start = (bf16[1792,896]{1,0:T(8,128)(2,1)S(1)}, bf16[1792,896]{1,0:T(8,128)(2,1)}, u32[]{:S(2)}) copy-start(bf16[1792,896]{1,0:T(8,128)(2,1)} %param.8) | copy-start | bytes 9633796
  145.4 45.8 %copy-start.1 = (s32[32]{0:T(128)S(1)}, s32[32]{0:T(128)}, u32[]{:S(2)}) copy-start(s32[32]{0:T(128)} %param.13) | copy-start | bytes 388
  145.4 47.1 %copy-start.2 = (s32[32]{0:T(128)S(1)}, s32[32]{0:T(128)}, u32[]{:S(2)}) copy-start(s32[32]{0:T(128)} %param.12) | copy-start | bytes 388
  145.4 47.8 %copy-start.3 = (s32[16]{0:T(128)S(1)}, s32[16]{0:T(128)}, u32[]{:S(2)}) copy-start(s32[16]{0:T(128)} %param.11) | copy-start | bytes 196

commit v8 on v6

--- a/solution.py
+++ b/solution.py
@@ -163,6 +163,85 @@
         ],
         compiler_params=pltpu.CompilerParams(collective_id=collective_id, has_side_effects=True),
     )(x.reshape((chips, 2) + block))
+
+
+def _route_kernel(x_ref, out_ref, send_buf, send_sems, recv_sems):
+    row = lax.axis_index("row")
+    col = lax.axis_index("col")
+    pairs = x_ref.shape[0] // 2
+    rows = lax.axis_size("row")
+    block = col // 2
+    half = lax.rem(col, 2)
+    base = pairs * half
+    source_col = 2 * row + col // pairs
+    mirrored = (row == block) & (col // pairs == half)
+
+    barrier = pltpu.get_barrier_semaphore()
+    for k in range(pairs):
+        target = base + k
+
+        @pl.when((block != row) | (target != col))
+        def _():
+            pl.semaphore_signal(barrier, inc=1, device_id=(block, target), device_id_type=pl.DeviceIdType.MESH)
+    for r in range(rows):
+
+        @pl.when((r != row) | (source_col != col))
+        def _():
+            pl.semaphore_signal(barrier, inc=1, device_id=(r, source_col), device_id_type=pl.DeviceIdType.MESH)
+
+    @pl.when(mirrored)
+    def _():
+        pl.semaphore_wait(barrier, pairs + rows - 2)
+
+    @pl.when(jnp.logical_not(mirrored))
+    def _():
+        pl.semaphore_wait(barrier, pairs + rows)
+
+    for k in range(pairs):
+        send_buf[k] = x_ref[2 * k:2 * k + 2, :]
+
+    def copy(k, r, device):
+        return pltpu.make_async_remote_copy(
+            src_ref=send_buf.at[k], dst_ref=out_ref.at[r], send_sem=send_sems.at[k], recv_sem=recv_sems.at[r],
+            device_id=device, device_id_type=pl.DeviceIdType.MESH)
+
+    for k in range(pairs):
+        target = base + k
+
+        @pl.when((block != row) | (target != col))
+        def _():
+            copy(k, row, (block, target)).start()
+
+        @pl.when((block == row) & (target == col))
+        def _():
+            out_ref[row] = send_buf[k]
+    for r in range(rows):
+
+        @pl.when((r != row) | (source_col != col))
+        def _():
+            copy(0, r, (r, source_col)).wait_recv()
+    for k in range(pairs):
+        target = base + k
+
+        @pl.when((block != row) | (target != col))
+        def _():
+            copy(k, row, (block, target)).wait_send()
+
+
+def route(x, rows, collective_id):
+    pairs = x.shape[0] // 2
+    return pl.pallas_call(
+        _route_kernel,
+        out_shape=jax.ShapeDtypeStruct((rows, 2, x.shape[1]), x.dtype),
+        in_specs=[pl.BlockSpec(memory_space=pltpu.VMEM)],
+        out_specs=pl.BlockSpec(memory_space=pltpu.VMEM),
+        scratch_shapes=[
+            pltpu.VMEM((pairs, 2, x.shape[1]), x.dtype),
+            pltpu.SemaphoreType.DMA((pairs,)),
+            pltpu.SemaphoreType.DMA((rows,)),
+        ],
+        compiler_params=pltpu.CompilerParams(collective_id=collective_id, has_side_effects=True),
+    )(x)
 
 
 def _ring_kernel(n, chunks, partial_ref, out_ref, recv_r, recv_l, acc_r, acc_l, rs_sems, ag_sems):
@@ -278,14 +357,13 @@
     )
     every_row = row_ring(partial_value.reshape(row_count, block_keys, -1), row_count, 3)
     whitened = every_row[row_index]
-    rows = every_row.reshape(row_count, col_count, part_keys, width)
-    terms = jnp.einsum("bcid,sjd->csbij", rows, stored_keys, preferred_element_type=jnp.float32)
-    terms = terms.reshape(col_count, local_batches * row_count * part_keys, batch_keys)
+    terms = jnp.einsum("brd,sjd->brsj", every_row.reshape(row_count, block_keys, width), stored_keys,
+                       preferred_element_type=jnp.float32)
+    terms = terms.reshape(col_count, block_keys // 2, local_batches * batch_keys)
     mine = col_scatter(terms, col_count, 1)
-    mine = mine.reshape(local_batches, row_count, part_keys, batch_keys).transpose(1, 0, 2, 3)
-    mine = mine.reshape(row_count, local_batches * part_keys, batch_keys)
-    routed = exchange(mine, "row", "col", row_count, False, 2)
-    table = routed.reshape(row_count * local_batches, part_keys, batch_keys)
+    routed = route(mine, row_count, 2)
+    table = routed.reshape(row_count, part_keys, local_batches, batch_keys).transpose(0, 2, 1, 3)
+    table = table.reshape(row_count * local_batches, part_keys, batch_keys)
     listed = pair_batch[row_index]
     slots = batch_slot[listed]
     lengths = batch_length[listed]

time: 196 us -> 198 us (1.010)
  Pallas kernels: 164 us -> 171 us
  local copies, waits for them, and re-layouts: 18.1 us -> 11.9 us
    pallas_call x1, Pallas kernels: 14.2 us -> 22.4 us  [route(): pl.pallas_call(_route_kernel, out_shape=jax.ShapeDtypeStruct((rows, 2, x....]
    reshape x5 -> x1, local copies, waits for them, and re-layouts: 7.26 us -> 0.05 us  [shards(): table = table.reshape(row_count * local_batches, part_keys, batch_keys)]
    dot_general x0 -> x1, local copies, waits for them, and re-layouts: none -> 2.95 us  [shards(): jnp.einsum('brd,sjd->brsj', every_row.reshape(row_count, block_keys, widt...]
    transpose x1 -> x0, local copies, waits for them, and re-layouts: 2.93 us -> none  [shards(): jnp.einsum('bcid,sjd->csbij', rows, stored_keys, preferred_element_type=j...]
where the time goes in v8:
time: 198 us; the launch traced here: 197 us
  Pallas kernels  171 us (86%)
  local copies, waits for them, and re-layouts  11.9 us (6%)
  matrix products  10.8 us (5%)
  other arithmetic  2.21 us (1%)
    pallas_call x1, Pallas kernels, row_ring(): pl.pallas_call(functools.partial(_ring_kernel, n, chunks), out_shape=jax....  80.5 us
    pallas_call x1, Pallas kernels, col_gather(): pl.pallas_call(functools.partial(_gather_kernel, n), out_shape=jax.ShapeD...  39.1 us
    pallas_call x1, Pallas kernels, col_scatter(): pl.pallas_call(functools.partial(_scatter_kernel, n), out_shape=jax.Shape...  29.4 us
    pallas_call x1, Pallas kernels, route(): pl.pallas_call(_route_kernel, out_shape=jax.ShapeDtypeStruct((rows, 2, x....  22.4 us
    dot_general x1, matrix products, shards(): jnp.dot(gathered.reshape(total_keys, new_keys.shape[1]), precision, prefe...  7.77 us
    another operation x1, local copies, waits for them, and re-layouts, col_scatter(): x.reshape((chips, 2) + block)  3.96 us

profile of v8, /device:TPU:1, one launch (start us, length us, event | category | flops | bytes accessed | tf_op | source)
XLA Modules:
  0.0 197.1 jit_solution(8840242712262698346)
XLA Ops:
  0.6 0.0 copy-start
  0.6 39.1 %shard_map.86 = bf16[32,32,1792]{2,1,0:T(8,128)(2,1)} custom-call(bf16[32,1792]{1,0:T(8,128)(2,1)} %x_ref.1), custom_call_target="tpu_custom_call" | custom-call | tf_op jit(solution)/shard_map/pallas_call | solution.py:96
  39.8 0.0 copy-done
  39.8 7.8 %fusion.partial_ref = f32[16,64,896]{2,1,0:T(8,128)} fusion(bf16[16,64,1792]{2,1,0:T(8,128)(2,1)} %bitcast.28, bf16[1792,896]{1,0:T(8,128)(2,1)S(1)} %copy-done), kind=kOutput, calls=%fused_computation.3 | convolution fusion | flops 3288334336 | bytes 10551296 | tf_op jit(solution)/shard_map/dot_general | solution.py:353
  47.5 80.5 %shard_map.87 = bf16[16,64,896]{2,1,0:T(8,128)(2,1)} custom-call(f32[16,64,896]{2,1,0:T(8,128)} %fusion.partial_ref), custom_call_target="tpu_custom_call" | custom-call | tf_op jit(solution)/shard_map/pallas_call | solution.py:327
  128.0 1.6 dynamic-slice_bitcast_fusion
  129.6 3.0 %fusion.2 = f32[16,64,2,256]{3,1,2,0:T(8,128)S(1)} fusion(bf16[16,64,896]{2,1,0:T(8,128)(2,1)} %shard_map.87, bf16[2,256,896]{2,1,0:T(8,128)(2,1)} %param.9), kind=kOutput, calls=%fused_computation.5 | convolution fusion | flops 939524096 | bytes 4849664 | tf_op jit(solution)/shard_map/brd,sjd->brsj/dot_general | solution.py:360
  132.6 2.9 %copy.10 = f32[16,64,2,256]{3,2,1,0:T(2,128)} copy(f32[16,64,2,256]{3,1,2,0:T(8,128)S(1)} %fusion.2) | data formatting | bytes 4194304 | tf_op jit(solution)/shard_map/brd,sjd->brsj/dot_general | solution.py:360
  135.6 0.0 copy-start.1
  135.6 0.0 copy-start.2
  135.6 0.0 copy-start.3
  135.6 4.0 %reshape_reshape.3.x_ref = f32[16,2,32,512]{3,2,1,0:T(8,128)} reshape(f32[16,64,2,256]{3,2,1,0:T(2,128)} %copy.10) | data formatting | bytes 4194304 | tf_op jit(solution)/shard_map/reshape;reshape | solution.py:165
  139.5 29.4 %shard_map.88.x_ref = f32[32,512]{1,0:T(8,128)} custom-call(f32[16,2,32,512]{3,2,1,0:T(8,128)} %reshape_reshape.3.x_ref), custom_call_target="tpu_custom_call" | custom-call | tf_op jit(solution)/shard_map/pallas_call | solution.py:152
  169.0 22.4 %shard_map.89 = f32[16,2,512]{2,1,0:T(2,128)} custom-call(f32[32,512]{1,0:T(8,128)} %shard_map.88.x_ref), custom_call_target="tpu_custom_call" | custom-call | tf_op jit(solution)/shard_map/pallas_call | solution.py:233
  191.4 0.8 fusion.9
  192.2 0.1 reshape.109
  192.3 0.7 fusion.7
  193.0 0.0 copy-done.1
  193.0 0.7 gather_fusion.1
  193.7 0.6 gather_fusion.2
  194.4 0.0 copy-done.2
  194.4 0.7 gather_fusion
  195.1 0.0 copy-done.3
  195.1 0.6 dynamic_slice.10
  195.7 0.6 iota_compare_fusion.1
  196.3 0.1 fusion.6
  196.4 0.7 fusion.5
  (5 shorter events, 0.1 us)
Async XLA Ops:
  0.6 39.1 %copy-start = (bf16[1792,896]{1,0:T(8,128)(2,1)S(1)}, bf16[1792,896]{1,0:T(8,128)(2,1)}, u32[]{:S(2)}) copy-start(bf16[1792,896]{1,0:T(8,128)(2,1)} %param.8) | copy-start | bytes 9633796
  135.6 57.4 %copy-start.1 = (s32[32]{0:T(128)S(1)}, s32[32]{0:T(128)}, u32[]{:S(2)}) copy-start(s32[32]{0:T(128)} %param.13) | copy-start | bytes 388
  135.6 58.8 %copy-start.2 = (s32[32]{0:T(128)S(1)}, s32[32]{0:T(128)}, u32[]{:S(2)}) copy-start(s32[32]{0:T(128)} %param.12) | copy-start | bytes 388
  135.6 59.5 %copy-start.3 = (s32[16]{0:T(128)S(1)}, s32[16]{0:T(128)}, u32[]{:S(2)}) copy-start(s32[16]{0:T(128)} %param.11) | copy-start | bytes 196

commit v9 on v8

--- a/solution.py
+++ b/solution.py
@@ -357,8 +357,8 @@
     )
     every_row = row_ring(partial_value.reshape(row_count, block_keys, -1), row_count, 3)
     whitened = every_row[row_index]
-    terms = jnp.einsum("brd,sjd->brsj", every_row.reshape(row_count, block_keys, width), stored_keys,
-                       preferred_element_type=jnp.float32)
+    terms = jnp.einsum("brd,kd->brk", every_row.reshape(row_count, block_keys, width),
+                       stored_keys.reshape(local_batches * batch_keys, width), preferred_element_type=jnp.float32)
     terms = terms.reshape(col_count, block_keys // 2, local_batches * batch_keys)
     mine = col_scatter(terms, col_count, 1)
     routed = route(mine, row_count, 2)

time: 198 us -> 192 us (0.970)
  local copies, waits for them, and re-layouts: 11.9 us -> 5.01 us
    another operation x1 -> x0, local copies, waits for them, and re-layouts: 3.96 us -> none  [col_scatter(): x.reshape((chips, 2) + block)]
    dot_general x1 -> x0, local copies, waits for them, and re-layouts: 2.95 us -> none  [shards(): jnp.einsum('brd,sjd->brsj', every_row.reshape(row_count, block_keys, widt...]
where the time goes in v9:
time: 192 us
  Pallas kernels  172 us (90%)
  matrix products  12.1 us (6%)
  local copies, waits for them, and re-layouts  5.01 us (3%)
  other arithmetic  2.21 us (1%)
    pallas_call x1, Pallas kernels, row_ring(): pl.pallas_call(functools.partial(_ring_kernel, n, chunks), out_shape=jax....  80.5 us
    pallas_call x1, Pallas kernels, col_gather(): pl.pallas_call(functools.partial(_gather_kernel, n), out_shape=jax.ShapeD...  39.1 us
    pallas_call x1, Pallas kernels, col_scatter(): pl.pallas_call(functools.partial(_scatter_kernel, n), out_shape=jax.Shape...  29.6 us
    pallas_call x1, Pallas kernels, route(): pl.pallas_call(_route_kernel, out_shape=jax.ShapeDtypeStruct((rows, 2, x....  22.5 us
    dot_general x1, matrix products, shards(): jnp.dot(gathered.reshape(total_keys, new_keys.shape[1]), precision, prefe...  7.77 us
    dot_general x1, matrix products, shards(): jnp.einsum('brd,kd->brk', every_row.reshape(row_count, block_keys, width)...  4.35 us

profile of v9, /device:TPU:1, one launch (start us, length us, event | category | flops | bytes accessed | tf_op | source)
XLA Modules:
  0.0 191.7 jit_solution(5134656376418712954)
XLA Ops:
  0.6 0.0 copy-start
  0.6 39.1 %shard_map.86 = bf16[32,32,1792]{2,1,0:T(8,128)(2,1)} custom-call(bf16[32,1792]{1,0:T(8,128)(2,1)} %x_ref.1), custom_call_target="tpu_custom_call" | custom-call | tf_op jit(solution)/shard_map/pallas_call | solution.py:96
  39.8 0.0 copy-done
  39.8 7.8 %fusion.partial_ref = f32[16,64,896]{2,1,0:T(8,128)} fusion(bf16[16,64,1792]{2,1,0:T(8,128)(2,1)} %bitcast.28, bf16[1792,896]{1,0:T(8,128)(2,1)S(1)} %copy-done), kind=kOutput, calls=%fused_computation.3 | convolution fusion | flops 3288334336 | bytes 10551296 | tf_op jit(solution)/shard_map/dot_general | solution.py:353
  47.5 80.5 %shard_map.87 = bf16[16,64,896]{2,1,0:T(8,128)(2,1)} custom-call(f32[16,64,896]{2,1,0:T(8,128)} %fusion.partial_ref), custom_call_target="tpu_custom_call" | custom-call | tf_op jit(solution)/shard_map/pallas_call | solution.py:327
  128.0 1.6 dynamic-slice_bitcast_fusion
  129.6 0.0 copy-start.1
  129.6 4.3 %fusion.7.x_ref = f32[16,2,32,512]{3,2,1,0:T(8,128)} fusion(bf16[16,2,32,896]{3,2,1,0:T(8,128)(2,1)} %bitcast.29, bf16[512,896,1,1]{1,0,3,2:T(8,128)(2,1)} %bitcast.30), kind=kOutput, calls=%fused_computation.21 | convolution fusion | flops 939524096 | bytes 4849664 | tf_op jit(solution)/shard_map/brd,kd->brk/dot_general | solution.py:360
  134.0 0.0 copy-start.2
  134.0 0.0 copy-start.3
  134.0 29.6 %shard_map.88.x_ref = f32[32,512]{1,0:T(8,128)} custom-call(f32[16,2,32,512]{3,2,1,0:T(8,128)} %fusion.7.x_ref), custom_call_target="tpu_custom_call" | custom-call | tf_op jit(solution)/shard_map/pallas_call | solution.py:152
  163.5 22.5 %shard_map.89 = f32[16,2,512]{2,1,0:T(2,128)} custom-call(f32[32,512]{1,0:T(8,128)} %shard_map.88.x_ref), custom_call_target="tpu_custom_call" | custom-call | tf_op jit(solution)/shard_map/pallas_call | solution.py:233
  186.0 0.8 fusion.6
  186.8 0.1 reshape.114
  186.9 0.7 fusion.4
  187.6 0.0 copy-done.1
  187.6 0.7 gather_fusion.1
  188.3 0.6 gather_fusion.2
  188.9 0.0 copy-done.2
  188.9 0.7 gather_fusion
  189.6 0.0 copy-done.3
  189.6 0.6 dynamic_slice.10
  190.2 0.6 iota_compare_fusion.1
  190.9 0.1 fusion.3
  191.0 0.7 fusion.2
  (5 shorter events, 0.1 us)
Async XLA Ops:
  0.6 39.1 %copy-start = (bf16[1792,896]{1,0:T(8,128)(2,1)S(1)}, bf16[1792,896]{1,0:T(8,128)(2,1)}, u32[]{:S(2)}) copy-start(bf16[1792,896]{1,0:T(8,128)(2,1)} %param.8) | copy-start | bytes 9633796
  129.6 58.0 %copy-start.1 = (s32[32]{0:T(128)S(1)}, s32[32]{0:T(128)}, u32[]{:S(2)}) copy-start(s32[32]{0:T(128)} %param.13) | copy-start | bytes 388
  134.0 55.0 %copy-start.2 = (s32[32]{0:T(128)S(1)}, s32[32]{0:T(128)}, u32[]{:S(2)}) copy-start(s32[32]{0:T(128)} %param.12) | copy-start | bytes 388
  134.0 55.7 %copy-start.3 = (s32[16]{0:T(128)S(1)}, s32[16]{0:T(128)}, u32[]{:S(2)}) copy-start(s32[16]{0:T(128)} %param.11) | copy-start | bytes 196

commit v10 on v9

--- a/solution.py
+++ b/solution.py
@@ -242,6 +242,124 @@
         ],
         compiler_params=pltpu.CompilerParams(collective_id=collective_id, has_side_effects=True),
     )(x)
+
+
+def _scatter_route_kernel(n, x_ref, out_ref, half_ref, recv, acc, summed, send_buf, send_sems, recv_sems,
+                          route_send, route_recv):
+    me = lax.axis_index("col")
+    row = lax.axis_index("row")
+    rows = lax.axis_size("row")
+    core = lax.rem(me, 2)
+    chip = me // 2
+    chips = n // 2
+    pairs = summed.shape[0] // 2
+    sibling = chip * 2 + 1 - core
+    peers = [lax.rem(chip + d, chips) * 2 + core for d in range(1, chips)]
+    block = me // 2
+    base = pairs * core
+    source_col = 2 * row + me // pairs
+    mirrored = (row == block) & (me // pairs == core)
+
+    barrier = pltpu.get_barrier_semaphore()
+    for peer in peers + [sibling]:
+        pl.semaphore_signal(barrier, inc=1, device_id=(row, peer), device_id_type=pl.DeviceIdType.MESH)
+    for k in range(pairs):
+        target = base + k
+
+        @pl.when((block != row) | (target != me))
+        def _():
+            pl.semaphore_signal(barrier, inc=1, device_id=(block, target), device_id_type=pl.DeviceIdType.MESH)
+    for r in range(rows):
+
+        @pl.when((r != row) | (source_col != me))
+        def _():
+            pl.semaphore_signal(barrier, inc=1, device_id=(r, source_col), device_id_type=pl.DeviceIdType.MESH)
+
+    @pl.when(mirrored)
+    def _():
+        pl.semaphore_wait(barrier, chips + pairs + rows - 2)
+
+    @pl.when(jnp.logical_not(mirrored))
+    def _():
+        pl.semaphore_wait(barrier, chips + pairs + rows)
+
+    swap = pltpu.make_async_remote_copy(
+        src_ref=x_ref.at[:, 1 - core], dst_ref=half_ref, send_sem=send_sems.at[0], recv_sem=recv_sems.at[0],
+        device_id=(row, sibling), device_id_type=pl.DeviceIdType.MESH)
+    swap.start()
+    swap.wait_recv()
+    acc[...] = x_ref[:, core] + half_ref[...]
+    sent = [swap]
+    for d in range(1, chips):
+        target = lax.rem(chip + d, chips)
+        c = pltpu.make_async_remote_copy(
+            src_ref=acc.at[target], dst_ref=recv.at[chip], send_sem=send_sems.at[d], recv_sem=recv_sems.at[d],
+            device_id=(row, target * 2 + core), device_id_type=pl.DeviceIdType.MESH)
+        c.start()
+        sent.append(c)
+    total = acc[chip]
+    for d in range(1, chips):
+        source = lax.rem(chip + chips - d, chips)
+        pltpu.make_async_remote_copy(
+            src_ref=acc.at[source], dst_ref=recv.at[source], send_sem=send_sems.at[d], recv_sem=recv_sems.at[d],
+            device_id=(row, source * 2 + core), device_id_type=pl.DeviceIdType.MESH).wait_recv()
+        total = total + recv[source]
+    summed[...] = total
+    for k in range(pairs):
+        send_buf[k] = summed[2 * k:2 * k + 2, :]
+
+    def copy(k, r, device):
+        return pltpu.make_async_remote_copy(
+            src_ref=send_buf.at[k], dst_ref=out_ref.at[r], send_sem=route_send.at[k], recv_sem=route_recv.at[r],
+            device_id=device, device_id_type=pl.DeviceIdType.MESH)
+
+    for k in range(pairs):
+        target = base + k
+
+        @pl.when((block != row) | (target != me))
+        def _():
+            copy(k, row, (block, target)).start()
+
+        @pl.when((block == row) & (target == me))
+        def _():
+            out_ref[row] = send_buf[k]
+    for r in range(rows):
+
+        @pl.when((r != row) | (source_col != me))
+        def _():
+            copy(0, r, (r, source_col)).wait_recv()
+    for k in range(pairs):
+        target = base + k
+
+        @pl.when((block != row) | (target != me))
+        def _():
+            copy(k, row, (block, target)).wait_send()
+    for c in sent:
+        c.wait_send()
+
+
+def scatter_route(x, n, rows, collective_id):
+    chips = n // 2
+    block = x.shape[1:]
+    pairs = block[0] // 2
+    return pl.pallas_call(
+        functools.partial(_scatter_route_kernel, n),
+        out_shape=jax.ShapeDtypeStruct((rows, 2, block[1]), x.dtype),
+        in_specs=[pl.BlockSpec(memory_space=pltpu.VMEM)],
+        out_specs=pl.BlockSpec(memory_space=pltpu.VMEM),
+        scratch_shapes=[
+            pltpu.VMEM((chips,) + block, x.dtype),
+            pltpu.VMEM((chips,) + block, x.dtype),
+            pltpu.VMEM((chips,) + block, x.dtype),
+            pltpu.VMEM(block, x.dtype),
+            pltpu.VMEM((pairs, 2, block[1]), x.dtype),
+            pltpu.SemaphoreType.DMA((chips,)),
+            pltpu.SemaphoreType.DMA((chips,)),
+            pltpu.SemaphoreType.DMA((pairs,)),
+            pltpu.SemaphoreType.DMA((rows,)),
+        ],
+        compiler_params=pltpu.CompilerParams(collective_id=collective_id, has_side_effects=True),
+    )(x.reshape((chips, 2) + block))
 
 
 def _ring_kernel(n, chunks, partial_ref, out_ref, recv_r, recv_l, acc_r, acc_l, rs_sems, ag_sems):
@@ -360,8 +478,7 @@
     terms = jnp.einsum("brd,kd->brk", every_row.reshape(row_count, block_keys, width),
                        stored_keys.reshape(local_batches * batch_keys, width), preferred_element_type=jnp.float32)
     terms = terms.reshape(col_count, block_keys // 2, local_batches * batch_keys)
-    mine = col_scatter(terms, col_count, 1)
-    routed = route(mine, row_count, 2)
+    routed = scatter_route(terms, col_count, row_count, 1)
     table = routed.reshape(row_count, part_keys, local_batches, batch_keys).transpose(0, 2, 1, 3)
     table = table.reshape(row_count * local_batches, part_keys, batch_keys)
     listed = pair_batch[row_index]

time: 192 us -> 188 us (0.979)
  Pallas kernels: 172 us -> 167 us
    pallas_call x2 -> x1, Pallas kernels: 52 us -> 47.7 us  [scatter_route(): pl.pallas_call(functools.partial(_scatter_route_kernel, n), out_shape=jax...]
where the time goes in v10:
time: 188 us; the launch traced here: 187 us
  Pallas kernels  167 us (89%)
  matrix products  12.1 us (6%)
  local copies, waits for them, and re-layouts  5.01 us (3%)
  other arithmetic  2.21 us (1%)
    pallas_call x1, Pallas kernels, row_ring(): pl.pallas_call(functools.partial(_ring_kernel, n, chunks), out_shape=jax....  80.5 us
    pallas_call x1, Pallas kernels, scatter_route(): pl.pallas_call(functools.partial(_scatter_route_kernel, n), out_shape=jax...  47.7 us
    pallas_call x1, Pallas kernels, col_gather(): pl.pallas_call(functools.partial(_gather_kernel, n), out_shape=jax.ShapeD...  39.1 us
    dot_general x1, matrix products, shards(): jnp.dot(gathered.reshape(total_keys, new_keys.shape[1]), precision, prefe...  7.77 us
    dot_general x1, matrix products, shards(): jnp.einsum('brd,kd->brk', every_row.reshape(row_count, block_keys, width)...  4.35 us

profile of v10, /device:TPU:1, one launch (start us, length us, event | category | flops | bytes accessed | tf_op | source)
XLA Modules:
  0.0 187.3 jit_solution(6173068768015810993)
XLA Ops:
  0.6 0.0 copy-start
  0.6 39.1 %shard_map.86 = bf16[32,32,1792]{2,1,0:T(8,128)(2,1)} custom-call(bf16[32,1792]{1,0:T(8,128)(2,1)} %x_ref.1), custom_call_target="tpu_custom_call" | custom-call | tf_op jit(solution)/shard_map/pallas_call | solution.py:96
  39.8 0.0 copy-done
  39.8 7.8 %fusion.partial_ref = f32[16,64,896]{2,1,0:T(8,128)} fusion(bf16[16,64,1792]{2,1,0:T(8,128)(2,1)} %bitcast.28, bf16[1792,896]{1,0:T(8,128)(2,1)S(1)} %copy-done), kind=kOutput, calls=%fused_computation.3 | convolution fusion | flops 3288334336 | bytes 10551296 | tf_op jit(solution)/shard_map/dot_general | solution.py:471
  47.5 80.5 %shard_map.87 = bf16[16,64,896]{2,1,0:T(8,128)(2,1)} custom-call(f32[16,64,896]{2,1,0:T(8,128)} %fusion.partial_ref), custom_call_target="tpu_custom_call" | custom-call | tf_op jit(solution)/shard_map/pallas_call | solution.py:445
  128.0 1.6 dynamic-slice_bitcast_fusion
  129.6 0.0 copy-start.1
  129.6 4.3 %fusion.7.x_ref = f32[16,2,32,512]{3,2,1,0:T(8,128)} fusion(bf16[16,2,32,896]{3,2,1,0:T(8,128)(2,1)} %bitcast.29, bf16[512,896,1,1]{1,0,3,2:T(8,128)(2,1)} %bitcast.30), kind=kOutput, calls=%fused_computation.21 | convolution fusion | flops 939524096 | bytes 4849664 | tf_op jit(solution)/shard_map/brd,kd->brk/dot_general | solution.py:478
  134.0 0.0 copy-start.2
  134.0 0.0 copy-start.3
  134.0 47.7 %shard_map.88 = f32[16,2,512]{2,1,0:T(2,128)} custom-call(f32[16,2,32,512]{3,2,1,0:T(8,128)} %fusion.7.x_ref), custom_call_target="tpu_custom_call" | custom-call | tf_op jit(solution)/shard_map/pallas_call | solution.py:345
  181.6 0.8 fusion.6
  182.5 0.1 reshape.114
  182.5 0.7 fusion.4
  183.2 0.0 copy-done.1
  183.2 0.7 gather_fusion.1
  183.9 0.6 gather_fusion.2
  184.6 0.0 copy-done.2
  184.6 0.7 gather_fusion
  185.3 0.0 copy-done.3
  185.3 0.6 dynamic_slice.10
  185.9 0.6 iota_compare_fusion.1
  186.5 0.1 fusion.3
  186.6 0.7 fusion.2
  (5 shorter events, 0.1 us)
Async XLA Ops:
  0.6 39.1 %copy-start = (bf16[1792,896]{1,0:T(8,128)(2,1)S(1)}, bf16[1792,896]{1,0:T(8,128)(2,1)}, u32[]{:S(2)}) copy-start(bf16[1792,896]{1,0:T(8,128)(2,1)} %param.8) | copy-start | bytes 9633796
  129.6 53.6 %copy-start.1 = (s32[32]{0:T(128)S(1)}, s32[32]{0:T(128)}, u32[]{:S(2)}) copy-start(s32[32]{0:T(128)} %param.13) | copy-start | bytes 388
  134.0 50.6 %copy-start.2 = (s32[32]{0:T(128)S(1)}, s32[32]{0:T(128)}, u32[]{:S(2)}) copy-start(s32[32]{0:T(128)} %param.12) | copy-start | bytes 388
  134.0 51.3 %copy-start.3 = (s32[16]{0:T(128)S(1)}, s32[16]{0:T(128)}, u32[]{:S(2)}) copy-start(s32[16]{0:T(128)} %param.11) | copy-start | bytes 196

commit v11 on v10

--- a/solution.py
+++ b/solution.py
@@ -362,19 +362,26 @@
     )(x.reshape((chips, 2) + block))
 
 
-def _ring_kernel(n, chunks, partial_ref, out_ref, recv_r, recv_l, acc_r, acc_l, rs_sems, ag_sems):
+def _ring_kernel(n, chunks, keys_ref, weights_ref, out_ref, own_ref, partial_ref, recv_r, recv_l, acc_r, acc_l,
+                 rs_sems, ag_sems):
     me = lax.axis_index("row")
     mine = lax.axis_index("col")
     right = lax.rem(me + 1, n)
     left = lax.rem(me + n - 1, n)
     steps_r = n // 2
     steps_l = n - 1 - steps_r
-    size = partial_ref.shape[1] // chunks
+    block = partial_ref.shape[1]
+    size = block // chunks
     half = n * chunks
     barrier = pltpu.get_barrier_semaphore()
     for peer in (left, right):
         pl.semaphore_signal(barrier, inc=1, device_id=(peer, mine), device_id_type=pl.DeviceIdType.MESH)
     pl.semaphore_wait(barrier, 2)
+
+    def whiten(d):
+        start = pl.multiple_of(d * block, block)
+        partial_ref[d] = jnp.dot(keys_ref[pl.ds(start, block), :], weights_ref[...],
+                                 preferred_element_type=jnp.float32)
 
     def send(src, dst, sems, k, peer):
         copy = pltpu.make_async_remote_copy(
@@ -387,9 +394,13 @@
     got_r = {}
     got_l = {}
     for s in range(steps_r):
+        d_r = lax.rem(me + steps_r - s, n)
+        d_l = lax.rem(me + n - steps_l + s, n)
+        whiten(d_r)
+        if s < steps_l:
+            whiten(d_l)
         for h in range(chunks):
             rows = pl.ds(h * size, size)
-            d_r = lax.rem(me + steps_r - s, n)
             if s == 0:
                 src = partial_ref.at[d_r, rows]
             else:
@@ -399,7 +410,6 @@
             got_r[s, h] = send(src, recv_r.at[s, rows], rs_sems, s * chunks + h, right)
             sent.append(got_r[s, h])
             if s < steps_l:
-                d_l = lax.rem(me + n - steps_l + s, n)
                 if s == 0:
                     src = partial_ref.at[d_l, rows]
                 else:
@@ -408,12 +418,15 @@
                     src = acc_l.at[s - 1, rows]
                 got_l[s, h] = send(src, recv_l.at[s, rows], rs_sems, half + s * chunks + h, left)
                 sent.append(got_l[s, h])
+    whiten(me)
     for h in range(chunks):
         rows = pl.ds(h * size, size)
         got_r[steps_r - 1, h].wait_recv()
         got_l[steps_l - 1, h].wait_recv()
         total = partial_ref[me, rows] + recv_r[steps_r - 1, rows] + recv_l[steps_l - 1, rows]
-        out_ref[me, rows] = total.astype(out_ref.dtype)
+        rounded = total.astype(out_ref.dtype)
+        out_ref[me, rows] = rounded
+        own_ref[rows] = rounded
 
     ag_r = {}
     ag_l = {}
@@ -438,16 +451,19 @@
         c.wait_send()
 
 
-def row_ring(partial, n, collective_id, chunks=2):
-    blocks, rows, width = partial.shape
+def row_ring(keys, weights, n, collective_id, chunks=2):
+    rows = keys.shape[0] // n
+    width = weights.shape[1]
     steps_r = n // 2
     steps_l = n - 1 - steps_r
     return pl.pallas_call(
         functools.partial(_ring_kernel, n, chunks),
-        out_shape=jax.ShapeDtypeStruct((blocks, rows, width), jnp.bfloat16),
-        in_specs=[pl.BlockSpec(memory_space=pltpu.VMEM)],
-        out_specs=pl.BlockSpec(memory_space=pltpu.VMEM),
+        out_shape=(jax.ShapeDtypeStruct((n, rows, width), jnp.bfloat16),
+                   jax.ShapeDtypeStruct((rows, width), jnp.bfloat16)),
+        in_specs=[pl.BlockSpec(memory_space=pltpu.VMEM)] * 2,
+        out_specs=(pl.BlockSpec(memory_space=pltpu.VMEM), pl.BlockSpec(memory_space=pltpu.VMEM)),
         scratch_shapes=[
+            pltpu.VMEM((n, rows, width), jnp.float32),
             pltpu.VMEM((steps_r, rows, width), jnp.float32),
             pltpu.VMEM((steps_l, rows, width), jnp.float32),
             pltpu.VMEM((steps_r - 1, rows, width), jnp.float32),
@@ -456,7 +472,7 @@
             pltpu.SemaphoreType.DMA((4 * n * chunks,)),
         ],
         compiler_params=pltpu.CompilerParams(collective_id=collective_id, has_side_effects=True),
-    )(partial)
+    )(keys, weights)
 
 
 def shards(new_keys, precision, stored_keys, pair_batch, pair_count, batch_length, batch_slot):
@@ -468,13 +484,7 @@
     part_keys = block_keys // col_count
     local_batches, batch_keys, width = stored_keys.shape
     gathered = col_gather(new_keys, col_count, 0)
-    partial_value = jnp.dot(
-        gathered.reshape(total_keys, new_keys.shape[1]),
-        precision,
-        preferred_element_type=jnp.float32,
-    )
-    every_row = row_ring(partial_value.reshape(row_count, block_keys, -1), row_count, 3)
-    whitened = every_row[row_index]
+    every_row, whitened = row_ring(gathered.reshape(total_keys, new_keys.shape[1]), precision, row_count, 3)
     terms = jnp.einsum("brd,kd->brk", every_row.reshape(row_count, block_keys, width),
                        stored_keys.reshape(local_batches * batch_keys, width), preferred_element_type=jnp.float32)
     terms = terms.reshape(col_count, block_keys // 2, local_batches * batch_keys)

time: 188 us -> 181 us (0.963)
  matrix products: 12.1 us -> 4.13 us
  Pallas kernels: 167 us -> 169 us
    dot_general x1 -> x0, matrix products: 7.77 us -> none  [shards(): jnp.dot(gathered.reshape(total_keys, new_keys.shape[1]), precision, prefe...]
    pallas_call x1, Pallas kernels: 80.5 us -> 83.1 us  [row_ring(): pl.pallas_call(functools.partial(_ring_kernel, n, chunks), out_shape=(jax...]
where the time goes in v11:
time: 181 us
  Pallas kernels  169 us (93%)
  matrix products  4.13 us (2%)
  local copies, waits for them, and re-layouts  4.11 us (2%)
  other arithmetic  2.21 us (1%)
    pallas_call x1, Pallas kernels, row_ring(): pl.pallas_call(functools.partial(_ring_kernel, n, chunks), out_shape=(jax...  83.1 us
    pallas_call x1, Pallas kernels, scatter_route(): pl.pallas_call(functools.partial(_scatter_route_kernel, n), out_shape=jax...  47.5 us
    pallas_call x1, Pallas kernels, col_gather(): pl.pallas_call(functools.partial(_gather_kernel, n), out_shape=jax.ShapeD...  38.9 us
    dot_general x1, matrix products, shards(): jnp.einsum('brd,kd->brk', every_row.reshape(row_count, block_keys, width)...  4.13 us

profile of v11, /device:TPU:1, one launch (start us, length us, event | category | flops | bytes accessed | tf_op | source)
XLA Modules:
  0.0 180.7 jit_solution(3384807601976206561)
XLA Ops:
  0.6 0.0 copy-start
  0.6 38.9 %shard_map.86 = bf16[32,32,1792]{2,1,0:T(8,128)(2,1)} custom-call(bf16[32,1792]{1,0:T(8,128)(2,1)} %x_ref.1), custom_call_target="tpu_custom_call" | custom-call | tf_op jit(solution)/shard_map/pallas_call | solution.py:96
  39.6 83.1 %shard_map.87 = (bf16[16,64,896]{2,1,0:T(8,128)(2,1)}, bf16[64,896]{1,0:T(8,128)(2,1)}) custom-call(bf16[1024,1792]{1,0:T(8,128)(2,1)} %bitcast.23, bf16[1792,896]{1,0:T(8,128)(2,1)} %weights_ref.1), custom_call_target="tpu_custom_call" | custom-call | tf_op jit(solution)/shard_map/pallas_call | solution.py:459
  122.7 0.0 copy-done
  122.7 4.1 %fusion.5.x_ref = f32[16,2,32,512]{3,2,1,0:T(8,128)} fusion(bf16[16,2,32,896]{3,2,1,0:T(8,128)(2,1)} %bitcast.24, bf16[512,896,1,1]{1,0,3,2:T(8,128)(2,1)S(1)} %bitcast.22), kind=kOutput, calls=%fused_computation.18 | convolution fusion | flops 939524096 | bytes 4849664 | tf_op jit(solution)/shard_map/brd,kd->brk/dot_general | solution.py:488
  126.8 0.0 copy-start.1
  126.8 0.0 copy-start.2
  126.8 0.0 copy-start.4
  126.8 0.0 copy-start.3
  126.8 47.5 %shard_map.88 = f32[16,2,512]{2,1,0:T(2,128)} custom-call(f32[16,2,32,512]{3,2,1,0:T(8,128)} %fusion.5.x_ref), custom_call_target="tpu_custom_call" | custom-call | tf_op jit(solution)/shard_map/pallas_call | solution.py:345
  174.3 0.8 fusion.4
  175.1 0.1 reshape.114
  175.2 0.7 fusion.2
  175.9 0.0 copy-done.1
  175.9 0.7 gather_fusion.1
  176.6 0.6 gather_fusion.2
  177.3 0.0 copy-done.2
  177.3 0.7 gather_fusion
  178.0 0.0 copy-done.4
  178.0 0.6 dynamic_slice.6
  178.6 0.6 iota_compare_fusion.1
  179.2 0.1 fusion.1
  179.3 0.7 fusion
  180.0 0.0 copy-done.3
  180.0 0.6 copy.11
  (5 shorter events, 0.1 us)
Async XLA Ops:
  0.6 122.0 %copy-start = (bf16[2,256,896]{2,1,0:T(8,128)(2,1)S(1)}, bf16[2,256,896]{2,1,0:T(8,128)(2,1)}, u32[]{:S(2)}) copy-start(bf16[2,256,896]{2,1,0:T(8,128)(2,1)} %param.9) | copy-start | bytes 2752516
  126.8 49.1 %copy-start.1 = (s32[32]{0:T(128)S(1)}, s32[32]{0:T(128)}, u32[]{:S(2)}) copy-start(s32[32]{0:T(128)} %param.13) | copy-start | bytes 388
  126.8 50.5 %copy-start.2 = (s32[32]{0:T(128)S(1)}, s32[32]{0:T(128)}, u32[]{:S(2)}) copy-start(s32[32]{0:T(128)} %param.12) | copy-start | bytes 388
  126.8 51.2 %copy-start.4 = (s32[16]{0:T(128)S(1)}, s32[16]{0:T(128)}, u32[]{:S(2)}) copy-start(s32[16]{0:T(128)} %param.11) | copy-start | bytes 196
  126.8 53.2 %copy-start.3 = (bf16[64,896]{1,0:T(8,128)(2,1)S(1)}, bf16[64,896]{1,0:T(8,128)(2,1)}, u32[]{:S(2)}) copy-start(bf16[64,896]{1,0:T(8,128)(2,1)} %get-tuple-element.10) | copy-start | bytes 344068

commit v12 on v11

--- a/solution.py
+++ b/solution.py
@@ -362,7 +362,7 @@
     )(x.reshape((chips, 2) + block))
 
 
-def _ring_kernel(n, chunks, keys_ref, weights_ref, out_ref, own_ref, partial_ref, recv_r, recv_l, acc_r, acc_l,
+def _ring_kernel(n, chunks, keys_ref, weights_ref, stored_ref, terms_ref, own_ref, out_ref, partial_ref, recv_r, recv_l, acc_r, acc_l,
                  rs_sems, ag_sems):
     me = lax.axis_index("row")
     mine = lax.axis_index("col")
@@ -382,6 +382,10 @@
         start = pl.multiple_of(d * block, block)
         partial_ref[d] = jnp.dot(keys_ref[pl.ds(start, block), :], weights_ref[...],
                                  preferred_element_type=jnp.float32)
+
+    def intersect(b):
+        terms_ref[b] = lax.dot_general(out_ref[b], stored_ref[...], (((1,), (1,)), ((), ())),
+                                       preferred_element_type=jnp.float32)
 
     def send(src, dst, sems, k, peer):
         copy = pltpu.make_async_remote_copy(
@@ -444,25 +448,32 @@
                     ag_l[t - 1, h].wait_recv()
                 ag_l[t, h] = send(out_ref.at[b_l, rows], out_ref.at[b_l, rows], ag_sems, half + t * chunks + h, left)
                 sent.append(ag_l[t, h])
+        intersect(lax.rem(me + n - t, n))
+        if t and t < steps_l:
+            intersect(lax.rem(me + t, n))
     for h in range(chunks):
         ag_r[steps_r - 1, h].wait_recv()
         ag_l[steps_l - 1, h].wait_recv()
+    intersect(lax.rem(me + n - steps_r, n))
+    intersect(lax.rem(me + steps_l, n))
     for c in sent:
         c.wait_send()
 
 
-def row_ring(keys, weights, n, collective_id, chunks=2):
+def row_ring(keys, weights, stored, n, collective_id, chunks=2):
     rows = keys.shape[0] // n
     width = weights.shape[1]
+    slots = stored.shape[0]
     steps_r = n // 2
     steps_l = n - 1 - steps_r
     return pl.pallas_call(
         functools.partial(_ring_kernel, n, chunks),
-        out_shape=(jax.ShapeDtypeStruct((n, rows, width), jnp.bfloat16),
+        out_shape=(jax.ShapeDtypeStruct((n, rows, slots), jnp.float32),
                    jax.ShapeDtypeStruct((rows, width), jnp.bfloat16)),
-        in_specs=[pl.BlockSpec(memory_space=pltpu.VMEM)] * 2,
+        in_specs=[pl.BlockSpec(memory_space=pltpu.VMEM)] * 3,
         out_specs=(pl.BlockSpec(memory_space=pltpu.VMEM), pl.BlockSpec(memory_space=pltpu.VMEM)),
         scratch_shapes=[
+            pltpu.VMEM((n, rows, width), jnp.bfloat16),
             pltpu.VMEM((n, rows, width), jnp.float32),
             pltpu.VMEM((steps_r, rows, width), jnp.float32),
             pltpu.VMEM((steps_l, rows, width), jnp.float32),
@@ -472,7 +483,7 @@
             pltpu.SemaphoreType.DMA((4 * n * chunks,)),
         ],
         compiler_params=pltpu.CompilerParams(collective_id=collective_id, has_side_effects=True),
-    )(keys, weights)
+    )(keys, weights, stored)
 
 
 def shards(new_keys, precision, stored_keys, pair_batch, pair_count, batch_length, batch_slot):
@@ -484,9 +495,8 @@
     part_keys = block_keys // col_count
     local_batches, batch_keys, width = stored_keys.shape
     gathered = col_gather(new_keys, col_count, 0)
-    every_row, whitened = row_ring(gathered.reshape(total_keys, new_keys.shape[1]), precision, row_count, 3)
-    terms = jnp.einsum("brd,kd->brk", every_row.reshape(row_count, block_keys, width),
-                       stored_keys.reshape(local_batches * batch_keys, width), preferred_element_type=jnp.float32)
+    terms, whitened = row_ring(gathered.reshape(total_keys, new_keys.shape[1]), precision,
+                               stored_keys.reshape(local_batches * batch_keys, width), row_count, 3)
     terms = terms.reshape(col_count, block_keys // 2, local_batches * batch_keys)
     routed = scatter_route(terms, col_count, row_count, 1)
     table = routed.reshape(row_count, part_keys, local_batches, batch_keys).transpose(0, 2, 1, 3)

time: 181 us -> 178 us (0.983)
  matrix products: 4.13 us -> 0 us
    dot_general x1 -> x0, matrix products: 4.13 us -> none  [shards(): jnp.einsum('brd,kd->brk', every_row.reshape(row_count, block_keys, width)...]
where the time goes in v12:
time: 178 us; the launch traced here: 177 us
  Pallas kernels  170 us (96%)
  local copies, waits for them, and re-layouts  4.11 us (2%)
  other arithmetic  2.21 us (1%)
    pallas_call x1, Pallas kernels, row_ring(): pl.pallas_call(functools.partial(_ring_kernel, n, chunks), out_shape=(jax...  84.3 us
    pallas_call x1, Pallas kernels, scatter_route(): pl.pallas_call(functools.partial(_scatter_route_kernel, n), out_shape=jax...  46.5 us
    pallas_call x1, Pallas kernels, col_gather(): pl.pallas_call(functools.partial(_gather_kernel, n), out_shape=jax.ShapeD...  38.9 us

profile of v12, /device:TPU:1, one launch (start us, length us, event | category | flops | bytes accessed | tf_op | source)
XLA Modules:
  0.0 176.8 jit_solution(10972133462631452187)
XLA Ops:
  0.6 0.0 copy-start
  0.6 38.9 %shard_map.86 = bf16[32,32,1792]{2,1,0:T(8,128)(2,1)} custom-call(bf16[32,1792]{1,0:T(8,128)(2,1)} %x_ref.1), custom_call_target="tpu_custom_call" | custom-call | tf_op jit(solution)/shard_map/pallas_call | solution.py:96
  39.6 84.3 %shard_map.87 = (f32[16,64,512]{2,1,0:T(8,128)}, bf16[64,896]{1,0:T(8,128)(2,1)}) custom-call(bf16[1024,1792]{1,0:T(8,128)(2,1)} %bitcast.16, bf16[1792,896]{1,0:T(8,128)(2,1)} %weights_ref.1, bf16[512,896]{1,0:T(8,128)(2,1)} %bitcast.18), custom_call_target="tpu_custom_call" | custom-call | tf_op jit(solution)/shard_map/pallas_call | solution.py:469
  123.9 0.0 copy-start.1
  123.9 0.0 copy-start.3
  123.9 0.0 copy-start.2
  123.9 46.5 %shard_map.88 = f32[16,2,512]{2,1,0:T(2,128)} custom-call(f32[16,2,32,512]{3,2,1,0:T(8,128)} %bitcast.17), custom_call_target="tpu_custom_call" | custom-call | tf_op jit(solution)/shard_map/pallas_call | solution.py:345
  170.4 0.8 fusion.4
  171.2 0.1 reshape.113
  171.3 0.7 fusion.2
  172.0 0.0 copy-done
  172.0 0.7 gather_fusion.1
  172.7 0.6 gather_fusion.2
  173.4 0.0 copy-done.1
  173.4 0.7 gather_fusion
  174.1 0.0 copy-done.3
  174.1 0.6 dynamic_slice.6
  174.7 0.6 iota_compare_fusion.1
  175.3 0.1 fusion.1
  175.4 0.7 fusion
  176.1 0.0 copy-done.2
  176.1 0.6 copy.10
  (5 shorter events, 0.1 us)
Async XLA Ops:
  0.6 171.4 %copy-start = (s32[32]{0:T(128)S(1)}, s32[32]{0:T(128)}, u32[]{:S(2)}) copy-start(s32[32]{0:T(128)} %param.13) | copy-start | bytes 388
  123.9 49.5 %copy-start.1 = (s32[32]{0:T(128)S(1)}, s32[32]{0:T(128)}, u32[]{:S(2)}) copy-start(s32[32]{0:T(128)} %param.12) | copy-start | bytes 388
  123.9 50.2 %copy-start.3 = (s32[16]{0:T(128)S(1)}, s32[16]{0:T(128)}, u32[]{:S(2)}) copy-start(s32[16]{0:T(128)} %param.11) | copy-start | bytes 196
  123.9 52.2 %copy-start.2 = (bf16[64,896]{1,0:T(8,128)(2,1)S(1)}, bf16[64,896]{1,0:T(8,128)(2,1)}, u32[]{:S(2)}) copy-start(bf16[64,896]{1,0:T(8,128)(2,1)} %get-tuple-element.10) | copy-start | bytes 344068

commit v13 on v12

--- a/solution.py
+++ b/solution.py
@@ -360,6 +360,79 @@
         ],
         compiler_params=pltpu.CompilerParams(collective_id=collective_id, has_side_effects=True),
     )(x.reshape((chips, 2) + block))
+
+
+def _torus_gather_kernel(n, side, x_ref, out_ref, send_sems, recv_sems):
+    me = lax.axis_index("col")
+    mine = lax.axis_index("row")
+    core = lax.rem(me, 2)
+    chip = me // 2
+    chips = n // 2
+    across = lax.rem(chip, side)
+    down = chip // side
+    sibling = chip * 2 + 1 - core
+    width = x_ref.shape[1] // 2
+    x_peers = [(down * side + lax.rem(across + d, side)) * 2 + core for d in range(1, side)]
+    y_peers = [(lax.rem(down + d, chips // side) * side + across) * 2 + core for d in range(1, chips // side)]
+    barrier = pltpu.get_barrier_semaphore()
+    for peer in x_peers + y_peers + [sibling]:
+        pl.semaphore_signal(barrier, inc=1, device_id=(mine, peer), device_id_type=pl.DeviceIdType.MESH)
+    pl.semaphore_wait(barrier, len(x_peers) + len(y_peers) + 1)
+
+    count = [0]
+    sent = []
+
+    def push(slot, part, peer, src=None):
+        cols = pl.ds(part * width, width)
+        copy = pltpu.make_async_remote_copy(
+            src_ref=out_ref.at[slot, :, cols] if src is None else src, dst_ref=out_ref.at[slot, :, cols],
+            send_sem=send_sems.at[count[0]], recv_sem=recv_sems.at[slot * 2 + part],
+            device_id=(mine, peer), device_id_type=pl.DeviceIdType.MESH)
+        copy.start()
+        count[0] += 1
+        sent.append(copy)
+
+    def arrived(slot, part):
+        cols = pl.ds(part * width, width)
+        pltpu.make_async_remote_copy(
+            src_ref=out_ref.at[slot, :, cols], dst_ref=out_ref.at[slot, :, cols],
+            send_sem=send_sems.at[0], recv_sem=recv_sems.at[slot * 2 + part],
+            device_id=(mine, sibling), device_id_type=pl.DeviceIdType.MESH).wait_recv()
+
+    out_ref[me] = x_ref[...]
+    for part, first, second in ((0, x_peers, y_peers), (1, y_peers, x_peers)):
+        for peer in first + second + [sibling]:
+            push(me, part, peer, x_ref.at[:, pl.ds(part * width, width)])
+    for part, first, second in ((0, x_peers, y_peers), (1, y_peers, x_peers)):
+        for peer in first:
+            arrived(peer, part)
+            for other in second + [sibling]:
+                push(peer, part, other)
+    for part, first, second in ((0, x_peers, y_peers), (1, y_peers, x_peers)):
+        for peer in second:
+            for line in [peer] + [lax.rem(p + 2 * chips + peer - me, 2 * chips) for p in first]:
+                arrived(line, part)
+                push(line, part, sibling)
+    for slot_chip in range(chips):
+        for part in range(2):
+            arrived(slot_chip * 2 + 1 - core, part)
+    for c in sent:
+        c.wait_send()
+
+
+def torus_gather(x, n, side, collective_id):
+    sends = 4 * n
+    return pl.pallas_call(
+        functools.partial(_torus_gather_kernel, n, side),
+        out_shape=jax.ShapeDtypeStruct((n,) + x.shape, x.dtype),
+        in_specs=[pl.BlockSpec(memory_space=pltpu.VMEM)],
+        out_specs=pl.BlockSpec(memory_space=pltpu.VMEM),
+        scratch_shapes=[
+            pltpu.SemaphoreType.DMA((sends,)),
+            pltpu.SemaphoreType.DMA((2 * n,)),
+        ],
+        compiler_params=pltpu.CompilerParams(collective_id=collective_id, has_side_effects=True),
+    )(x)
 
 
 def _ring_kernel(n, chunks, keys_ref, weights_ref, stored_ref, terms_ref, own_ref, out_ref, partial_ref, recv_r, recv_l, acc_r, acc_l,
@@ -494,7 +567,7 @@
     block_keys = total_keys // row_count
     part_keys = block_keys // col_count
     local_batches, batch_keys, width = stored_keys.shape
-    gathered = col_gather(new_keys, col_count, 0)
+    gathered = torus_gather(new_keys, col_count, 4, 0)
     terms, whitened = row_ring(gathered.reshape(total_keys, new_keys.shape[1]), precision,
                                stored_keys.reshape(local_batches * batch_keys, width), row_count, 3)
     terms = terms.reshape(col_count, block_keys // 2, local_batches * batch_keys)

time: 178 us -> 168 us (0.944)
  Pallas kernels: 170 us -> 160 us
    pallas_call x1, Pallas kernels: 38.9 us -> 28.8 us  [torus_gather(): pl.pallas_call(functools.partial(_torus_gather_kernel, n, side), out_shap...]
where the time goes in v13:
time: 168 us; the launch traced here: 167 us
  Pallas kernels  160 us (95%)
  local copies, waits for them, and re-layouts  4.11 us (2%)
  other arithmetic  2.21 us (1%)
    pallas_call x1, Pallas kernels, row_ring(): pl.pallas_call(functools.partial(_ring_kernel, n, chunks), out_shape=(jax...  83.6 us
    pallas_call x1, Pallas kernels, scatter_route(): pl.pallas_call(functools.partial(_scatter_route_kernel, n), out_shape=jax...  47.8 us
    pallas_call x1, Pallas kernels, torus_gather(): pl.pallas_call(functools.partial(_torus_gather_kernel, n, side), out_shap...  28.8 us

profile of v13, /device:TPU:1, one launch (start us, length us, event | category | flops | bytes accessed | tf_op | source)
XLA Modules:
  0.0 167.2 jit_solution(16328601724125839748)
XLA Ops:
  0.6 0.0 copy-start
  0.6 28.8 %shard_map.86 = bf16[32,32,1792]{2,1,0:T(8,128)(2,1)} custom-call(bf16[32,1792]{1,0:T(8,128)(2,1)} %x_ref.1), custom_call_target="tpu_custom_call" | custom-call | tf_op jit(solution)/shard_map/pallas_call | solution.py:425
  29.4 83.6 %shard_map.87 = (f32[16,64,512]{2,1,0:T(8,128)}, bf16[64,896]{1,0:T(8,128)(2,1)}) custom-call(bf16[1024,1792]{1,0:T(8,128)(2,1)} %bitcast.16, bf16[1792,896]{1,0:T(8,128)(2,1)} %weights_ref.1, bf16[512,896]{1,0:T(8,128)(2,1)} %bitcast.18), custom_call_target="tpu_custom_call" | custom-call | tf_op jit(solution)/shard_map/pallas_call | solution.py:542
  113.0 0.0 copy-start.1
  113.0 0.0 copy-start.3
  113.0 0.0 copy-start.2
  113.0 47.8 %shard_map.88 = f32[16,2,512]{2,1,0:T(2,128)} custom-call(f32[16,2,32,512]{3,2,1,0:T(8,128)} %bitcast.17), custom_call_target="tpu_custom_call" | custom-call | tf_op jit(solution)/shard_map/pallas_call | solution.py:345
  160.9 0.8 fusion.4
  161.7 0.1 reshape.113
  161.7 0.7 fusion.2
  162.4 0.0 copy-done
  162.4 0.7 gather_fusion.1
  163.2 0.6 gather_fusion.2
  163.8 0.0 copy-done.1
  163.8 0.7 gather_fusion
  164.5 0.0 copy-done.3
  164.5 0.6 dynamic_slice.6
  165.1 0.6 iota_compare_fusion.1
  165.8 0.1 fusion.1
  165.8 0.7 fusion
  166.6 0.0 copy-done.2
  166.6 0.6 copy.10
  (5 shorter events, 0.1 us)
Async XLA Ops:
  0.6 161.8 %copy-start = (s32[32]{0:T(128)S(1)}, s32[32]{0:T(128)}, u32[]{:S(2)}) copy-start(s32[32]{0:T(128)} %param.13) | copy-start | bytes 388
  113.0 50.8 %copy-start.1 = (s32[32]{0:T(128)S(1)}, s32[32]{0:T(128)}, u32[]{:S(2)}) copy-start(s32[32]{0:T(128)} %param.12) | copy-start | bytes 388
  113.0 51.5 %copy-start.3 = (s32[16]{0:T(128)S(1)}, s32[16]{0:T(128)}, u32[]{:S(2)}) copy-start(s32[16]{0:T(128)} %param.11) | copy-start | bytes 196
  113.0 53.5 %copy-start.2 = (bf16[64,896]{1,0:T(8,128)(2,1)S(1)}, bf16[64,896]{1,0:T(8,128)(2,1)}, u32[]{:S(2)}) copy-start(bf16[64,896]{1,0:T(8,128)(2,1)} %get-tuple-element.10) | copy-start | bytes 344068

commit v14 on v13

--- a/solution.py
+++ b/solution.py
@@ -244,8 +244,8 @@
     )(x)
 
 
-def _scatter_route_kernel(n, x_ref, out_ref, half_ref, recv, acc, summed, send_buf, send_sems, recv_sems,
-                          route_send, route_recv):
+def _scatter_route_kernel(n, side, x_ref, out_ref, half_ref, recv_a, recv_b, part_sum, acc, summed, send_buf,
+                          send_sems, recv_sems, route_send, route_recv):
     me = lax.axis_index("col")
     row = lax.axis_index("row")
     rows = lax.axis_size("row")
@@ -254,7 +254,11 @@
     chips = n // 2
     pairs = summed.shape[0] // 2
     sibling = chip * 2 + 1 - core
-    peers = [lax.rem(chip + d, chips) * 2 + core for d in range(1, chips)]
+    across = lax.rem(chip, side)
+    down = chip // side
+    lines = chips // side
+    peers = [(down * side + lax.rem(across + d, side)) * 2 + core for d in range(1, side)]
+    peers += [(lax.rem(down + d, lines) * side + across) * 2 + core for d in range(1, lines)]
     block = me // 2
     base = pairs * core
     source_col = 2 * row + me // pairs
@@ -277,11 +281,11 @@
 
     @pl.when(mirrored)
     def _():
-        pl.semaphore_wait(barrier, chips + pairs + rows - 2)
+        pl.semaphore_wait(barrier, len(peers) + 1 + pairs + rows - 2)
 
     @pl.when(jnp.logical_not(mirrored))
     def _():
-        pl.semaphore_wait(barrier, chips + pairs + rows)
+        pl.semaphore_wait(barrier, len(peers) + 1 + pairs + rows)
 
     swap = pltpu.make_async_remote_copy(
         src_ref=x_ref.at[:, 1 - core], dst_ref=half_ref, send_sem=send_sems.at[0], recv_sem=recv_sems.at[0],
@@ -290,21 +294,56 @@
     swap.wait_recv()
     acc[...] = x_ref[:, core] + half_ref[...]
     sent = [swap]
-    for d in range(1, chips):
-        target = lax.rem(chip + d, chips)
+    width = acc.shape[2] // 2
+    count = [1]
+
+    def chip_at(y, x):
+        return y * side + x
+
+    def copy(src, dst, sem, peer_chip):
         c = pltpu.make_async_remote_copy(
-            src_ref=acc.at[target], dst_ref=recv.at[chip], send_sem=send_sems.at[d], recv_sem=recv_sems.at[d],
-            device_id=(row, target * 2 + core), device_id_type=pl.DeviceIdType.MESH)
-        c.start()
-        sent.append(c)
-    total = acc[chip]
-    for d in range(1, chips):
-        source = lax.rem(chip + chips - d, chips)
-        pltpu.make_async_remote_copy(
-            src_ref=acc.at[source], dst_ref=recv.at[source], send_sem=send_sems.at[d], recv_sem=recv_sems.at[d],
-            device_id=(row, source * 2 + core), device_id_type=pl.DeviceIdType.MESH).wait_recv()
-        total = total + recv[source]
-    summed[...] = total
+            src_ref=src, dst_ref=dst, send_sem=send_sems.at[count[0]], recv_sem=recv_sems.at[sem],
+            device_id=(row, peer_chip * 2 + core), device_id_type=pl.DeviceIdType.MESH)
+        return c
+
+    for part in range(2):
+        cols = pl.ds(part * width, width)
+        mine_first, mine_second = (across, down) if part == 0 else (down, across)
+        size_first, size_second = (side, lines) if part == 0 else (lines, side)
+
+        def place(first, second):
+            return chip_at(second, first) if part == 0 else chip_at(first, second)
+
+        for d in range(1, size_first):
+            far = lax.rem(mine_first + d, size_first)
+            for k in range(size_second):
+                c = copy(acc.at[place(far, k), :, cols], recv_a.at[part, mine_first, k],
+                         16 + part * 16 + mine_first * 4 + k, place(far, mine_second))
+                c.start()
+                count[0] += 1
+                sent.append(c)
+        for d in range(1, size_first):
+            near = lax.rem(mine_first + size_first - d, size_first)
+            for k in range(size_second):
+                copy(acc.at[0, :, cols], recv_a.at[part, near, k], 16 + part * 16 + near * 4 + k, 0).wait_recv()
+        for k in range(size_second):
+            total = acc[place(mine_first, k), :, cols]
+            for d in range(1, size_first):
+                total = total + recv_a[part, lax.rem(mine_first + d, size_first), k]
+            part_sum[part, k] = total
+        for d in range(1, size_second):
+            far = lax.rem(mine_second + d, size_second)
+            c = copy(part_sum.at[part, far], recv_b.at[part, mine_second], 48 + part * 4 + mine_second,
+                     place(mine_first, far))
+            c.start()
+            count[0] += 1
+            sent.append(c)
+        total = part_sum[part, mine_second]
+        for d in range(1, size_second):
+            near = lax.rem(mine_second + size_second - d, size_second)
+            copy(part_sum.at[part, 0], recv_b.at[part, near], 48 + part * 4 + near, 0).wait_recv()
+            total = total + recv_b[part, near]
+        summed[:, cols] = total
     for k in range(pairs):
         send_buf[k] = summed[2 * k:2 * k + 2, :]
 
@@ -338,23 +377,27 @@
         c.wait_send()
 
 
-def scatter_route(x, n, rows, collective_id):
+def scatter_route(x, n, rows, collective_id, side=4):
     chips = n // 2
     block = x.shape[1:]
     pairs = block[0] // 2
+    lines = chips // side
+    width = block[1] // 2
     return pl.pallas_call(
-        functools.partial(_scatter_route_kernel, n),
+        functools.partial(_scatter_route_kernel, n, side),
         out_shape=jax.ShapeDtypeStruct((rows, 2, block[1]), x.dtype),
         in_specs=[pl.BlockSpec(memory_space=pltpu.VMEM)],
         out_specs=pl.BlockSpec(memory_space=pltpu.VMEM),
         scratch_shapes=[
             pltpu.VMEM((chips,) + block, x.dtype),
-            pltpu.VMEM((chips,) + block, x.dtype),
+            pltpu.VMEM((2, max(side, lines), max(side, lines), block[0], width), x.dtype),
+            pltpu.VMEM((2, max(side, lines), block[0], width), x.dtype),
+            pltpu.VMEM((2, max(side, lines), block[0], width), x.dtype),
             pltpu.VMEM((chips,) + block, x.dtype),
             pltpu.VMEM(block, x.dtype),
             pltpu.VMEM((pairs, 2, block[1]), x.dtype),
-            pltpu.SemaphoreType.DMA((chips,)),
-            pltpu.SemaphoreType.DMA((chips,)),
+            pltpu.SemaphoreType.DMA((64,)),
+            pltpu.SemaphoreType.DMA((64,)),
             pltpu.SemaphoreType.DMA((pairs,)),
             pltpu.SemaphoreType.DMA((rows,)),
         ],

time: 168 us -> 175 us (1.042)
  Pallas kernels: 160 us -> 167 us
    pallas_call x1, Pallas kernels: 47.8 us -> 54.8 us  [scatter_route(): pl.pallas_call(functools.partial(_scatter_route_kernel, n, side), out_sha...]
where the time goes in v14:
time: 175 us; the launch traced here: 174 us
  Pallas kernels  167 us (95%)
  local copies, waits for them, and re-layouts  4.11 us (2%)
  other arithmetic  2.21 us (1%)
    pallas_call x1, Pallas kernels, row_ring(): pl.pallas_call(functools.partial(_ring_kernel, n, chunks), out_shape=(jax...  83.6 us
    pallas_call x1, Pallas kernels, scatter_route(): pl.pallas_call(functools.partial(_scatter_route_kernel, n, side), out_sha...  54.8 us
    pallas_call x1, Pallas kernels, torus_gather(): pl.pallas_call(functools.partial(_torus_gather_kernel, n, side), out_shap...  28.8 us

profile of v14, /device:TPU:1, one launch (start us, length us, event | category | flops | bytes accessed | tf_op | source)
XLA Modules:
  0.0 174.2 jit_solution(15368955436798877025)
XLA Ops:
  0.6 0.0 copy-start
  0.6 28.8 %shard_map.86 = bf16[32,32,1792]{2,1,0:T(8,128)(2,1)} custom-call(bf16[32,1792]{1,0:T(8,128)(2,1)} %x_ref.1), custom_call_target="tpu_custom_call" | custom-call | tf_op jit(solution)/shard_map/pallas_call | solution.py:468
  29.4 83.6 %shard_map.87 = (f32[16,64,512]{2,1,0:T(8,128)}, bf16[64,896]{1,0:T(8,128)(2,1)}) custom-call(bf16[1024,1792]{1,0:T(8,128)(2,1)} %bitcast.16, bf16[1792,896]{1,0:T(8,128)(2,1)} %weights_ref.1, bf16[512,896]{1,0:T(8,128)(2,1)} %bitcast.18), custom_call_target="tpu_custom_call" | custom-call | tf_op jit(solution)/shard_map/pallas_call | solution.py:585
  113.0 0.0 copy-start.1
  113.0 0.0 copy-start.3
  113.0 0.0 copy-start.2
  113.0 54.8 %shard_map.88 = f32[16,2,512]{2,1,0:T(2,128)} custom-call(f32[16,2,32,512]{3,2,1,0:T(8,128)} %bitcast.17), custom_call_target="tpu_custom_call" | custom-call | tf_op jit(solution)/shard_map/pallas_call | solution.py:386
  167.8 0.8 fusion.4
  168.7 0.1 reshape.113
  168.7 0.7 fusion.2
  169.4 0.0 copy-done
  169.4 0.7 gather_fusion.1
  170.2 0.6 gather_fusion.2
  170.8 0.0 copy-done.1
  170.8 0.7 gather_fusion
  171.5 0.0 copy-done.3
  171.5 0.6 dynamic_slice.6
  172.1 0.6 iota_compare_fusion.1
  172.8 0.1 fusion.1
  172.8 0.7 fusion
  173.6 0.0 copy-done.2
  173.6 0.6 copy.10
  (5 shorter events, 0.1 us)
Async XLA Ops:
  0.6 168.8 %copy-start = (s32[32]{0:T(128)S(1)}, s32[32]{0:T(128)}, u32[]{:S(2)}) copy-start(s32[32]{0:T(128)} %param.13) | copy-start | bytes 388
  113.0 57.8 %copy-start.1 = (s32[32]{0:T(128)S(1)}, s32[32]{0:T(128)}, u32[]{:S(2)}) copy-start(s32[32]{0:T(128)} %param.12) | copy-start | bytes 388
  113.0 58.5 %copy-start.3 = (s32[16]{0:T(128)S(1)}, s32[16]{0:T(128)}, u32[]{:S(2)}) copy-start(s32[16]{0:T(128)} %param.11) | copy-start | bytes 196
  113.0 60.5 %copy-start.2 = (bf16[64,896]{1,0:T(8,128)(2,1)S(1)}, bf16[64,896]{1,0:T(8,128)(2,1)}, u32[]{:S(2)}) copy-start(bf16[64,896]{1,0:T(8,128)(2,1)} %get-tuple-element.10) | copy-start | bytes 344068

commit v15 on v13

--- a/solution.py
+++ b/solution.py
@@ -574,15 +574,19 @@
     routed = scatter_route(terms, col_count, row_count, 1)
     table = routed.reshape(row_count, part_keys, local_batches, batch_keys).transpose(0, 2, 1, 3)
     table = table.reshape(row_count * local_batches, part_keys, batch_keys)
-    listed = pair_batch[row_index]
-    slots = batch_slot[listed]
-    lengths = batch_length[listed]
-    count = pair_count[row_index]
-    picked = jnp.take(table, slots, axis=0)
-    places = jnp.arange(slots.shape[0], dtype=jnp.int32)
+    listed = lax.dynamic_index_in_dim(pair_batch, row_index, 0, keepdims=False)
+    count = lax.dynamic_index_in_dim(pair_count, row_index, 0, keepdims=False)
+    places = jnp.arange(listed.shape[0], dtype=jnp.int32)
+    batches = jnp.arange(batch_slot.shape[0], dtype=jnp.int32)
+    hit = (listed[:, None] == batches[None, :]) & (places < count)[:, None]
+    lengths = jnp.sum(jnp.where(hit, batch_length[None, :], 0), axis=1)
+    choose = jnp.where(hit[:, :, None] & (batch_slot[None, :, None] == batches[None, None, :]), 1.0, 0.0)
+    choose = jnp.sum(choose, axis=1)
+    picked = jnp.einsum("ps,sk->pk", choose, table.reshape(table.shape[0], -1),
+                        precision=lax.Precision.HIGHEST, preferred_element_type=jnp.float32)
+    picked = picked.reshape(listed.shape[0], part_keys, batch_keys)
     columns = jnp.arange(batch_keys, dtype=jnp.int32)
-    keep = (places < count)[:, None, None] & (columns[None, None, :] < lengths[:, None, None])
-    shares = jnp.where(keep, picked, jnp.zeros_like(picked))
+    shares = jnp.where(columns[None, None, :] < lengths[:, None, None], picked, 0.0)
     return (whitened, shares[None])
 
 

time: 168 us -> 166 us (0.988)
    gather x3 -> x0, local copies, waits for them, and re-layouts: 2.01 us -> none  [the longest x1 0.7 us: shards(): lengths = batch_length[listed]]
where the time goes in v15:
time: 166 us
  Pallas kernels  160 us (96%)
  local copies, waits for them, and re-layouts  2.83 us (2%)
    pallas_call x1, Pallas kernels, row_ring(): pl.pallas_call(functools.partial(_ring_kernel, n, chunks), out_shape=(jax...  83.7 us
    pallas_call x1, Pallas kernels, scatter_route(): pl.pallas_call(functools.partial(_scatter_route_kernel, n), out_shape=jax...  47.4 us
    pallas_call x1, Pallas kernels, torus_gather(): pl.pallas_call(functools.partial(_torus_gather_kernel, n, side), out_shap...  28.8 us

profile of v15, /device:TPU:1, one launch (start us, length us, event | category | flops | bytes accessed | tf_op | source)
XLA Modules:
  0.0 165.7 jit_solution(5982589248782265584)
XLA Ops:
  0.6 0.0 copy-start
  0.6 28.8 %shard_map.86 = bf16[32,32,1792]{2,1,0:T(8,128)(2,1)} custom-call(bf16[32,1792]{1,0:T(8,128)(2,1)} %x_ref.1), custom_call_target="tpu_custom_call" | custom-call | tf_op jit(solution)/shard_map/pallas_call | solution.py:425
  29.4 0.0 copy-start.3
  29.4 0.0 copy-start.2
  29.5 0.0 copy-start.1
  29.5 83.7 %shard_map.87 = (f32[16,64,512]{2,1,0:T(8,128)}, bf16[64,896]{1,0:T(8,128)(2,1)}) custom-call(bf16[1024,1792]{1,0:T(8,128)(2,1)} %bitcast.26, bf16[1792,896]{1,0:T(8,128)(2,1)} %weights_ref.1, bf16[512,896]{1,0:T(8,128)(2,1)} %bitcast.28), custom_call_target="tpu_custom_call" | custom-call | tf_op jit(solution)/shard_map/pallas_call | solution.py:542
  113.2 0.0 copy-done.3
  113.2 0.6 dynamic_slice.9
  113.8 0.6 iota_compare_fusion.3
  114.4 0.0 copy-done
  114.4 0.0 copy-done.2
  114.5 0.2 select_reduce_fusion.1
  114.6 0.1 iota_compare_fusion
  114.7 0.0 copy-done.1
  114.7 0.1 iota_compare_fusion.1
  114.8 0.1 fusion.4
  114.9 0.2 select_reduce_fusion
  115.1 47.4 %shard_map.88 = f32[16,2,512]{2,1,0:T(2,128)} custom-call(f32[16,2,32,512]{3,2,1,0:T(8,128)} %bitcast.27), custom_call_target="tpu_custom_call" | custom-call | tf_op jit(solution)/shard_map/pallas_call | solution.py:345
  162.5 1.0 fusion
  163.5 0.6 copy.15
  164.2 1.6 copy.26
  (1 shorter events, 0.0 us)
Async XLA Ops:
  0.6 113.8 %copy-start = (s32[16,24]{1,0:T(8,128)S(1)}, s32[16,24]{1,0:T(8,128)}, u32[]{:S(2)}) copy-start(s32[16,24]{1,0:T(8,128)} %param.10) | copy-start | bytes 4612
  29.4 83.7 %copy-start.3 = (s32[16]{0:T(128)S(1)}, s32[16]{0:T(128)}, u32[]{:S(2)}) copy-start(s32[16]{0:T(128)} %param.11) | copy-start | bytes 196
  29.4 85.0 %copy-start.2 = (s32[32]{0:T(128)S(1)}, s32[32]{0:T(128)}, u32[]{:S(2)}) copy-start(s32[32]{0:T(128)} %param.12) | copy-start | bytes 388
  29.5 85.3 %copy-start.1 = (s32[32]{0:T(128)S(1)}, s32[32]{0:T(128)}, u32[]{:S(2)}) copy-start(s32[32]{0:T(128)} %param.13) | copy-start | bytes 388

commit v16 on v15

--- a/solution.py
+++ b/solution.py
@@ -501,9 +501,8 @@
         got_r[steps_r - 1, h].wait_recv()
         got_l[steps_l - 1, h].wait_recv()
         total = partial_ref[me, rows] + recv_r[steps_r - 1, rows] + recv_l[steps_l - 1, rows]
-        rounded = total.astype(out_ref.dtype)
-        out_ref[me, rows] = rounded
-        own_ref[rows] = rounded
+        out_ref[me, rows] = total.astype(out_ref.dtype)
+        own_ref[rows] = total
 
     ag_r = {}
     ag_l = {}
@@ -542,7 +541,7 @@
     return pl.pallas_call(
         functools.partial(_ring_kernel, n, chunks),
         out_shape=(jax.ShapeDtypeStruct((n, rows, slots), jnp.float32),
-                   jax.ShapeDtypeStruct((rows, width), jnp.bfloat16)),
+                   jax.ShapeDtypeStruct((rows, width), jnp.float32)),
         in_specs=[pl.BlockSpec(memory_space=pltpu.VMEM)] * 3,
         out_specs=(pl.BlockSpec(memory_space=pltpu.VMEM), pl.BlockSpec(memory_space=pltpu.VMEM)),
         scratch_shapes=[
@@ -570,6 +569,7 @@
     gathered = torus_gather(new_keys, col_count, 4, 0)
     terms, whitened = row_ring(gathered.reshape(total_keys, new_keys.shape[1]), precision,
                                stored_keys.reshape(local_batches * batch_keys, width), row_count, 3)
+    whitened = whitened.astype(jnp.bfloat16)
     terms = terms.reshape(col_count, block_keys // 2, local_batches * batch_keys)
     routed = scatter_route(terms, col_count, row_count, 1)
     table = routed.reshape(row_count, part_keys, local_batches, batch_keys).transpose(0, 2, 1, 3)
@@ -582,9 +582,8 @@
     lengths = jnp.sum(jnp.where(hit, batch_length[None, :], 0), axis=1)
     choose = jnp.where(hit[:, :, None] & (batch_slot[None, :, None] == batches[None, None, :]), 1.0, 0.0)
     choose = jnp.sum(choose, axis=1)
-    picked = jnp.einsum("ps,sk->pk", choose, table.reshape(table.shape[0], -1),
+    picked = jnp.einsum("ps,sik->pik", choose, table,
                         precision=lax.Precision.HIGHEST, preferred_element_type=jnp.float32)
-    picked = picked.reshape(listed.shape[0], part_keys, batch_keys)
     columns = jnp.arange(batch_keys, dtype=jnp.int32)
     shares = jnp.where(columns[None, None, :] < lengths[:, None, None], picked, 0.0)
     return (whitened, shares[None])

time: 166 us -> 166 us (level)
  no operation moved by 1% of the time
where the time goes in v16:
time: 166 us
  Pallas kernels  160 us (96%)
  other arithmetic  2.89 us (2%)
  local copies, waits for them, and re-layouts  2.11 us (1%)
    pallas_call x1, Pallas kernels, row_ring(): pl.pallas_call(functools.partial(_ring_kernel, n, chunks), out_shape=(jax...  83.7 us
    pallas_call x1, Pallas kernels, scatter_route(): pl.pallas_call(functools.partial(_scatter_route_kernel, n), out_shape=jax...  47.5 us
    pallas_call x1, Pallas kernels, torus_gather(): pl.pallas_call(functools.partial(_torus_gather_kernel, n, side), out_shap...  28.8 us

profile of v16, /device:TPU:1, one launch (start us, length us, event | category | flops | bytes accessed | tf_op | source)
XLA Modules:
  0.0 166.0 jit_solution(4379289145676760416)
XLA Ops:
  0.6 0.0 copy-start
  0.6 28.8 %shard_map.86 = bf16[32,32,1792]{2,1,0:T(8,128)(2,1)} custom-call(bf16[32,1792]{1,0:T(8,128)(2,1)} %x_ref.1), custom_call_target="tpu_custom_call" | custom-call | tf_op jit(solution)/shard_map/pallas_call | solution.py:425
  29.4 0.0 copy-start.3
  29.4 0.0 copy-start.2
  29.5 0.0 copy-start.1
  29.5 83.7 %shard_map.87 = (f32[16,64,512]{2,1,0:T(8,128)}, f32[64,896]{1,0:T(8,128)}) custom-call(bf16[1024,1792]{1,0:T(8,128)(2,1)} %bitcast.11, bf16[1792,896]{1,0:T(8,128)(2,1)} %weights_ref.1, bf16[512,896]{1,0:T(8,128)(2,1)} %bitcast.13), custom_call_target="tpu_custom_call" | custom-call | tf_op jit(solution)/shard_map/pallas_call | solution.py:541
  113.2 1.6 convert_element_type.3
  114.8 47.5 %shard_map.88 = f32[16,2,512]{2,1,0:T(2,128)} custom-call(f32[16,2,32,512]{3,2,1,0:T(8,128)} %bitcast.12), custom_call_target="tpu_custom_call" | custom-call | tf_op jit(solution)/shard_map/pallas_call | solution.py:345
  162.3 0.8 fusion.4
  163.1 0.1 reshape.104
  163.2 0.0 copy-done.3
  163.2 0.6 dynamic_slice.9
  163.8 0.6 iota_compare_fusion.3
  164.5 0.0 copy-done
  164.5 0.0 copy-done.2
  164.5 0.2 select_reduce_fusion.1
  164.7 0.1 iota_compare_fusion
  164.8 0.0 copy-done.1
  164.8 0.1 iota_compare_fusion.1
  164.8 0.1 fusion.3
  164.9 0.2 select_reduce_fusion
  165.1 0.2 fusion
  165.3 0.6 copy.12
  (2 shorter events, 0.0 us)
Async XLA Ops:
  0.6 163.8 %copy-start = (s32[16,24]{1,0:T(8,128)S(1)}, s32[16,24]{1,0:T(8,128)}, u32[]{:S(2)}) copy-start(s32[16,24]{1,0:T(8,128)} %param.10) | copy-start | bytes 4612
  29.4 133.8 %copy-start.3 = (s32[16]{0:T(128)S(1)}, s32[16]{0:T(128)}, u32[]{:S(2)}) copy-start(s32[16]{0:T(128)} %param.11) | copy-start | bytes 196
  29.4 135.1 %copy-start.2 = (s32[32]{0:T(128)S(1)}, s32[32]{0:T(128)}, u32[]{:S(2)}) copy-start(s32[32]{0:T(128)} %param.12) | copy-start | bytes 388
  29.5 135.3 %copy-start.1 = (s32[32]{0:T(128)S(1)}, s32[32]{0:T(128)}, u32[]{:S(2)}) copy-start(s32[32]{0:T(128)} %param.13) | copy-start | bytes 388

commit v17 on v15

--- a/solution.py
+++ b/solution.py
@@ -134,7 +134,8 @@
             device_id=(mine, target * 2 + core), device_id_type=pl.DeviceIdType.MESH)
         c.start()
         sent.append(c)
-    total = acc[chip]
+    swap(chip).wait_recv()
+    total = x_ref[chip, core] + half_ref[chip]
     for d in range(1, chips):
         source = lax.rem(chip + chips - d, chips)
         pltpu.make_async_remote_copy(
@@ -245,7 +246,7 @@
 
 
 def _scatter_route_kernel(n, x_ref, out_ref, half_ref, recv, acc, summed, send_buf, send_sems, recv_sems,
-                          route_send, route_recv):
+                          route_send, route_recv, swap_send, swap_recv):
     me = lax.axis_index("col")
     row = lax.axis_index("row")
     rows = lax.axis_size("row")
@@ -283,21 +284,27 @@
     def _():
         pl.semaphore_wait(barrier, chips + pairs + rows)
 
-    swap = pltpu.make_async_remote_copy(
-        src_ref=x_ref.at[:, 1 - core], dst_ref=half_ref, send_sem=send_sems.at[0], recv_sem=recv_sems.at[0],
-        device_id=(row, sibling), device_id_type=pl.DeviceIdType.MESH)
-    swap.start()
-    swap.wait_recv()
-    acc[...] = x_ref[:, core] + half_ref[...]
-    sent = [swap]
+    def swap(k):
+        return pltpu.make_async_remote_copy(
+            src_ref=x_ref.at[k, 1 - core], dst_ref=half_ref.at[k], send_sem=swap_send.at[k], recv_sem=swap_recv.at[k],
+            device_id=(row, sibling), device_id_type=pl.DeviceIdType.MESH)
+
+    sent = []
+    for d in list(range(1, chips)) + [0]:
+        c = swap(lax.rem(chip + d, chips))
+        c.start()
+        sent.append(c)
     for d in range(1, chips):
         target = lax.rem(chip + d, chips)
+        swap(target).wait_recv()
+        acc[target] = x_ref[target, core] + half_ref[target]
         c = pltpu.make_async_remote_copy(
             src_ref=acc.at[target], dst_ref=recv.at[chip], send_sem=send_sems.at[d], recv_sem=recv_sems.at[d],
             device_id=(row, target * 2 + core), device_id_type=pl.DeviceIdType.MESH)
         c.start()
         sent.append(c)
-    total = acc[chip]
+    swap(chip).wait_recv()
+    total = x_ref[chip, core] + half_ref[chip]
     for d in range(1, chips):
         source = lax.rem(chip + chips - d, chips)
         pltpu.make_async_remote_copy(
@@ -357,6 +364,8 @@
             pltpu.SemaphoreType.DMA((chips,)),
             pltpu.SemaphoreType.DMA((pairs,)),
             pltpu.SemaphoreType.DMA((rows,)),
+            pltpu.SemaphoreType.DMA((chips,)),
+            pltpu.SemaphoreType.DMA((chips,)),
         ],
         compiler_params=pltpu.CompilerParams(collective_id=collective_id, has_side_effects=True),
     )(x.reshape((chips, 2) + block))

time: 166 us -> 165 us (level)
  no operation moved by 1% of the time
where the time goes in v17:
time: 165 us
  Pallas kernels  159 us (96%)
  local copies, waits for them, and re-layouts  2.83 us (2%)
    pallas_call x1, Pallas kernels, row_ring(): pl.pallas_call(functools.partial(_ring_kernel, n, chunks), out_shape=(jax...  83.7 us
    pallas_call x1, Pallas kernels, scatter_route(): pl.pallas_call(functools.partial(_scatter_route_kernel, n), out_shape=jax...  46.5 us
    pallas_call x1, Pallas kernels, torus_gather(): pl.pallas_call(functools.partial(_torus_gather_kernel, n, side), out_shap...  28.8 us

profile of v17, /device:TPU:1, one launch (start us, length us, event | category | flops | bytes accessed | tf_op | source)
XLA Modules:
  0.0 164.8 jit_solution(196698955092684218)
XLA Ops:
  0.6 0.0 copy-start
  0.6 28.8 %shard_map.86 = bf16[32,32,1792]{2,1,0:T(8,128)(2,1)} custom-call(bf16[32,1792]{1,0:T(8,128)(2,1)} %x_ref.1), custom_call_target="tpu_custom_call" | custom-call | tf_op jit(solution)/shard_map/pallas_call | solution.py:434
  29.4 0.0 copy-start.3
  29.4 0.0 copy-start.2
  29.5 0.0 copy-start.1
  29.5 83.7 %shard_map.87 = (f32[16,64,512]{2,1,0:T(8,128)}, bf16[64,896]{1,0:T(8,128)(2,1)}) custom-call(bf16[1024,1792]{1,0:T(8,128)(2,1)} %bitcast.26, bf16[1792,896]{1,0:T(8,128)(2,1)} %weights_ref.1, bf16[512,896]{1,0:T(8,128)(2,1)} %bitcast.28), custom_call_target="tpu_custom_call" | custom-call | tf_op jit(solution)/shard_map/pallas_call | solution.py:551
  113.2 0.0 copy-done.3
  113.2 0.6 dynamic_slice.9
  113.8 0.6 iota_compare_fusion.3
  114.4 0.0 copy-done
  114.4 0.0 copy-done.2
  114.5 0.2 select_reduce_fusion.1
  114.6 0.1 iota_compare_fusion
  114.7 0.0 copy-done.1
  114.7 0.1 iota_compare_fusion.1
  114.8 0.1 fusion.4
  114.9 0.2 select_reduce_fusion
  115.1 46.5 %shard_map.88 = f32[16,2,512]{2,1,0:T(2,128)} custom-call(f32[16,2,32,512]{3,2,1,0:T(8,128)} %bitcast.27), custom_call_target="tpu_custom_call" | custom-call | tf_op jit(solution)/shard_map/pallas_call | solution.py:352
  161.6 1.0 fusion
  162.6 0.6 copy.15
  163.3 1.6 copy.26
  (1 shorter events, 0.0 us)
Async XLA Ops:
  0.6 113.8 %copy-start = (s32[16,24]{1,0:T(8,128)S(1)}, s32[16,24]{1,0:T(8,128)}, u32[]{:S(2)}) copy-start(s32[16,24]{1,0:T(8,128)} %param.10) | copy-start | bytes 4612
  29.4 83.7 %copy-start.3 = (s32[16]{0:T(128)S(1)}, s32[16]{0:T(128)}, u32[]{:S(2)}) copy-start(s32[16]{0:T(128)} %param.11) | copy-start | bytes 196
  29.4 85.0 %copy-start.2 = (s32[32]{0:T(128)S(1)}, s32[32]{0:T(128)}, u32[]{:S(2)}) copy-start(s32[32]{0:T(128)} %param.12) | copy-start | bytes 388
  29.5 85.3 %copy-start.1 = (s32[32]{0:T(128)S(1)}, s32[32]{0:T(128)}, u32[]{:S(2)}) copy-start(s32[32]{0:T(128)} %param.13) | copy-start | bytes 388
